TPU v7x, 32 devices: a whole 2x2x4 slice. The times are simulated.
32 devices in a mesh: ens: 2 (over y), space: 4 (over z), tm: 2 (over x), mom: 2 (over core).
Axes of the slice: x: 2, y: 2, z: 4, core: 2. Of those that a mesh axis runs over, the one named last changes fastest.
Arguments:
- eigvecs: bfloat16 [8, 2, 3, 256, 2048], P(('ens', 'tm'), None, None, None, 'space'), parts along dimension 0, may hold values from -0.359375 to 0.359375
- momenta: int32 [4, 3], P('mom'), may hold values from 1 to 2
- pairs: int32 [2, 2], replicated, may hold values from 0 to 3, as said below
- spin_weights: float32 [4, 4], replicated, may hold values from -1 to 1
- perambulators: bfloat16 [4, 2, 4, 4, 256, 256], P(('ens', 'tm'), None, None, None, 'space'), parts along dimension 0, may hold values from -0.0234375 to 0.0234375
Outputs:
- blocks: bfloat16 [4, 4, 2, 256, 256], P(('ens', 'tm'), 'mom', None, 'space'), parts along dimension 0
There are 2 independent parts, one for each index of `ens`. A program takes and returns all parts, laid end to end along the dimension named above; an argument that names none is the same for every part. Nothing has to cross between parts.
Inputs may be any that keep to these rules, and one draw needn't show every extreme that they name: pairs[q, 0], the sink, lies in time group q: (q) * 2 <= pairs[q, 0] < (q + 1) * 2; pairs[q, 1], the source, is any timeslice.
All inputs are finite; a program needn't handle non-finite values.
Results may differ from a plain program's by a relative error of at most 0.008.
Values may be sent and summed in bfloat16 or wider, within the bound.
No kernel may reach another device: no remote copies, remote signals or barrier semaphores. Data moves between devices by JAX's collectives and lax.ppermute only.
A program may use at most 64 MiB of HBM per device.

v0:
```python
import math

import jax
import jax.numpy as jnp
from jax import lax
from jax.sharding import PartitionSpec as P

LAT = 48


EXACT_PRECISION = lax.Precision.HIGHEST


def phases(momenta, site_ids):
    xcoord = (site_ids % LAT).astype(jnp.float32)
    ycoord = (site_ids // LAT % LAT).astype(jnp.float32)
    zcoord = (site_ids // (LAT * LAT)).astype(jnp.float32)
    mom_float = momenta.astype(jnp.float32)
    angles = (
        mom_float[:, 0:1] * xcoord + mom_float[:, 1:2] * ycoord + mom_float[:, 2:3] * zcoord
    ) * (2.0 * math.pi / LAT)
    return (jnp.cos(angles), jnp.sin(angles))


def elemental_terms(eigvecs, cosine_rows, sine_rows):
    contract_dims = (((0, 2), (0, 2)), ((), ()))
    per_time = []
    for which_time in range(eigvecs.shape[0]):
        real_vec = eigvecs[which_time, 0]
        imag_vec = eigvecs[which_time, 1]
        real_wide = real_vec.astype(jnp.float32)
        imag_wide = imag_vec.astype(jnp.float32)
        per_mom = []
        for which_mom in range(cosine_rows.shape[0]):
            cosine = cosine_rows[which_mom]
            sine = sine_rows[which_mom]
            real_turned = (cosine * real_wide + sine * imag_wide).astype(jnp.bfloat16)
            imag_turned = (cosine * imag_wide - sine * real_wide).astype(jnp.bfloat16)
            real_part = lax.dot_general(
                real_vec, real_turned, contract_dims, preferred_element_type=jnp.float32
            ) + lax.dot_general(
                imag_vec, imag_turned, contract_dims, preferred_element_type=jnp.float32
            )
            imag_part = lax.dot_general(
                real_vec, imag_turned, contract_dims, preferred_element_type=jnp.float32
            ) - lax.dot_general(
                imag_vec, real_turned, contract_dims, preferred_element_type=jnp.float32
            )
            per_mom.append(jnp.stack([real_part, imag_part]))
        per_time.append(jnp.stack(per_mom))
    return jnp.stack(per_time)


def source_slots(held_rows, pairs, my_group, times_dev, tm_size, pair_dev):
    wanted = pairs[:, 1].reshape(tm_size, pair_dev)
    local_times = jnp.arange(times_dev, dtype=jnp.int32) + my_group * times_dev
    chosen = (wanted[:, :, None] == local_times).astype(jnp.bfloat16)
    return jnp.einsum(
        "rqt,tmcij->rqmcij", chosen, held_rows, preferred_element_type=jnp.float32
    ).astype(jnp.bfloat16)


def sink_select(held_rows, my_pairs, my_group, times_dev):
    local_times = jnp.arange(times_dev, dtype=jnp.int32) + my_group * times_dev
    chosen = (my_pairs[:, 0][:, None] == local_times).astype(jnp.bfloat16)
    return jnp.einsum(
        "qt,tmcij->qmcij", chosen, held_rows, preferred_element_type=jnp.float32
    ).astype(jnp.bfloat16)


def bridge(mixed_block, source):
    real_part = jnp.einsum(
        "qkl,qmjl->qmkj", mixed_block[:, 0], source[:, :, 0], preferred_element_type=jnp.float32
    ) + jnp.einsum(
        "qkl,qmjl->qmkj", mixed_block[:, 1], source[:, :, 1], preferred_element_type=jnp.float32
    )
    imag_part = jnp.einsum(
        "qkl,qmjl->qmkj", mixed_block[:, 1], source[:, :, 0], preferred_element_type=jnp.float32
    ) - jnp.einsum(
        "qkl,qmjl->qmkj", mixed_block[:, 0], source[:, :, 1], preferred_element_type=jnp.float32
    )
    return jnp.stack([real_part, imag_part], 2).astype(jnp.bfloat16)


def attach(sink_elem, bridged):
    real_part = jnp.einsum(
        "qmik,qmkj->qmij", sink_elem[:, :, 0], bridged[:, :, 0], preferred_element_type=jnp.float32
    ) - jnp.einsum(
        "qmik,qmkj->qmij", sink_elem[:, :, 1], bridged[:, :, 1], preferred_element_type=jnp.float32
    )
    imag_part = jnp.einsum(
        "qmik,qmkj->qmij", sink_elem[:, :, 0], bridged[:, :, 1], preferred_element_type=jnp.float32
    ) + jnp.einsum(
        "qmik,qmkj->qmij", sink_elem[:, :, 1], bridged[:, :, 0], preferred_element_type=jnp.float32
    )
    return jnp.stack([real_part, imag_part], 2)


def local(eigvecs, momenta, pairs, spin_weights, perambulators):
    times_dev = eigvecs.shape[0]
    vec_count = eigvecs.shape[3]
    sites_dev = eigvecs.shape[4]
    pair_dev = perambulators.shape[0]
    tm_size = lax.axis_size("tm")
    space_size = lax.axis_size("space")
    my_group = lax.axis_index("tm")
    my_place = lax.axis_index("space")
    rows_dev = vec_count // space_size
    row_first = my_place * rows_dev
    site_ids = my_place * sites_dev + jnp.arange(sites_dev, dtype=jnp.int32)
    cosine_rows, sine_rows = phases(momenta, site_ids)
    partial_value = elemental_terms(eigvecs, cosine_rows, sine_rows)
    my_pairs = lax.dynamic_slice_in_dim(pairs, my_group * pair_dev, pair_dev, 0)
    whole = lax.psum(partial_value, "space").astype(jnp.bfloat16)
    outgoing = source_slots(whole, pairs, my_group, times_dev, tm_size, pair_dev)
    arrived = lax.all_to_all(outgoing, "tm", split_axis=0, concat_axis=0, tiled=True)
    source_full = jnp.sum(arrived, axis=0, dtype=jnp.float32).astype(jnp.bfloat16)
    sink_whole = sink_select(whole, my_pairs, my_group, times_dev)
    sink_own = lax.dynamic_slice_in_dim(sink_whole, row_first, rows_dev, 3)
    mixed_peramb = jnp.einsum(
        "ab,qcabkl->qckl",
        spin_weights,
        perambulators.astype(jnp.float32),
        precision=EXACT_PRECISION,
    ).astype(jnp.bfloat16)
    bridged = bridge(lax.all_gather(mixed_peramb, "space", axis=2, tiled=True), source_full)
    blocks = attach(sink_own, bridged).astype(jnp.bfloat16)
    return blocks


def solution(mesh):
    return jax.shard_map(
        local,
        mesh=mesh,
        in_specs=(
            P(("ens", "tm"), None, None, None, "space"),
            P("mom", None),
            P(),
            P(),
            P(("ens", "tm"), None, None, None, "space", None),
        ),
        out_specs=P(("ens", "tm"), "mom", None, "space", None),
        check_vma=False,
    )
```

profile of v0, /device:TPU:0, one launch (start us, length us, event | category | flops | bytes accessed | tf_op | source)
XLA Modules:
  0.0 120.1 jit_solution(8111220607492806430)
XLA Ops:
  0.0 0.8 convert_element_type.166
  1.3 2.2 %convolution_bitcast_fusion.14 = f32[256,256]{1,0:T(8,128)S(1)} fusion(f32[512]{0:T(512)S(1)} %bitcast.288, f32[512]{0:T(512)S(1)} %bitcast.296, bf16[2,2,3,256,512]{4,3,2,1,0:T(8,128)(2,1)} %param.5), kind=kOutput, calls=%fused_computation.55 | convolution fusion | flops 203685888 | bytes 2625536 | tf_op jit(solution)/shard_map/dot_general | solution.py:41
  3.5 0.4 copy-done.1
  3.9 0.4 convolution_bitcast_fusion.12
  4.3 0.5 convolution_bitcast_fusion.10
  4.8 0.4 convolution_bitcast_fusion.8
  5.2 0.4 convolution_bitcast_fusion.6
  5.7 0.5 convolution_bitcast_fusion.4
  6.1 0.5 convolution_bitcast_fusion.2
  6.6 0.4 convolution_bitcast_fusion
  7.1 0.4 fusion.22
  7.5 0.5 fusion.24
  8.0 0.5 fusion.26
  8.4 0.5 fusion.28
  8.9 0.5 fusion.30
  9.4 0.5 fusion.32
  9.8 0.5 fusion.34
  10.3 0.5 fusion.36
  11.2 79.3 %all-reduce.1 = bf16[2,2,2,256,256]{3,4,2,1,0:T(8,128)(2,1)} all-reduce(f32[2,2,2,256,256]{3,4,2,1,0:T(8,128)S(1)} %pad_maximum_fusion), channel_id=1, replica_groups=mesh['ens'=2,'space'=4,'tm'=2,'mom'=2] {'space'}, use_global_device_ids=true, to_apply=%region_0.1 | all-reduce | flops 524288 | bytes 3145728 | tf_op jit(solution)/shard_map/psum | solution.py:114
  90.5 2.5 %copy.12 = bf16[2,2,2,256,256]{4,0,3,2,1:T(2,128)(2,1)S(1)} copy(bf16[2,2,2,256,256]{3,4,2,1,0:T(8,128)(2,1)} %all-reduce.1) | data formatting | bytes 2097152 | tf_op jit(solution)/shard_map/convert_element_type | solution.py:114
  93.3 1.3 %fusion.16 = bf16[2,1,2,2,256,256]{5,0,4,3,2,1:T(2,128)(2,1)S(1)} fusion(bf16[2,2,2,256,256]{4,0,3,2,1:T(2,128)(2,1)S(1)} %copy.12, s32[2]{0:T(128)S(1)} %iota_add_fusion.1, s32[2]{0:T(128)S(1)} %slice_reduce_fusion), kind=kOutput, calls=%fused_computation.34 | convolution fusion | flops 2621444 | bytes 2097168 | tf_op jit(solution)/shard_map/rqt,tmcij->rqmcij/dot_general | solution.py:58
  94.6 1.1 copy.13
  95.7 3.9 %all-to-all-start = ((bf16[2,1,2,2,256,256]{5,4,3,2,1,0:T(8,128)(2,1)}), bf16[2,1,2,2,256,256]{5,4,3,2,1,0:T(8,128)(2,1)S(1)}, u32[]{:S(2)}, u32[]{:S(2)}) async-start(bf16[2,1,2,2,256,256]{5,4,3,2,1,0:T(8,128)(2,1)} %copy.13), calls=%async_computation | async-start | bytes 2097152 | tf_op jit(solution)/shard_map/all_to_all | solution.py:116
  99.6 2.1 %fusion.41 = bf16[1,2,64,256,1]{3,0,4,2,1:T(2,128)(2,1)S(1)} fusion(f32[4,4,1,1,1]{1,2,0,4,3:T(1,128)S(1)} %bitcast.304, bf16[2,4,4,64,256]{4,3,2,1,0:T(8,128)(2,1)S(1)} %bitcast.261), kind=kOutput, calls=%fused_computation.82 | convolution fusion | flops 6291456 | bytes 1114176 | tf_op jit(solution)/shard_map/ab,qcabkl->qckl/dot_general | solution.py:120
  101.8 1.3 %fusion.145 = bf16[1,2,2,256,256]{4,0,3,2,1:T(2,128)(2,1)S(1)} fusion(bf16[2,2,2,256,256]{4,0,3,2,1:T(2,128)(2,1)S(1)} %copy.12, s32[]{:T(128)S(1)} %bitcast.305, s32[]{:T(128)S(6)} %mul.205), kind=kOutput, calls=%fused_computation.194 | convolution fusion | flops 1048580 | bytes 1572872 | tf_op jit(solution)/shard_map/qt,tmcij->qmcij/dot_general | solution.py:66
  103.1 13.8 %all-gather = bf16[2,256,256]{2,1,0:T(8,128)(2,1)S(1)} all-gather(bf16[2,64,256]{2,1,0:T(8,128)(2,1)S(1)} %bitcast.271), channel_id=2, replica_groups=mesh['ens'=2,'space'=4,'tm'=2,'mom'=2] {'space'}, dimensions={1}, use_global_device_ids=true | all-gather | bytes 327680 | tf_op jit(solution)/shard_map/all_gather | solution.py:126
  116.9 0.5 reduce_sum.14
  117.5 0.2 fusion.100
  117.7 0.3 fusion.99
  118.0 0.3 fusion.20
  118.3 0.3 fusion.19
  119.4 0.7 copy.20
  (34 shorter events, 2.1 us)
Async XLA Ops:
  0.0 99.6 %copy-start = (bf16[1,2,4,4,64,256]{5,4,3,2,1,0:T(8,128)(2,1)S(1)}, bf16[1,2,4,4,64,256]{5,4,3,2,1,0:T(8,128)(2,1)}, u32[]{:S(2)}) copy-start(bf16[1,2,4,4,64,256]{5,4,3,2,1,0:T(8,128)(2,1)} %param.9) | copy-start | bytes 3145732
  1.3 2.6 %copy-start.1 = (bf16[2,2,3,256,512]{4,3,2,1,0:T(8,128)(2,1)S(1)}, bf16[2,2,3,256,512]{4,3,2,1,0:T(8,128)(2,1)}, u32[]{:S(2)}) copy-start(bf16[2,2,3,256,512]{4,3,2,1,0:T(8,128)(2,1)} %param.5) | copy-start | bytes 9437188
  90.5 2.6 %copy-start.3 = (s32[2,2]{1,0:T(2,128)S(1)}, s32[2,2]{1,0:T(2,128)}, u32[]{:S(2)}) copy-start(s32[2,2]{1,0:T(2,128)} %param.7) | copy-start | bytes 52
  95.7 3.9 %copy-start.2 = (f32[4,4]{1,0:T(4,128)S(1)}, f32[4,4]{1,0:T(4,128)}, u32[]{:S(2)}) copy-start(f32[4,4]{1,0:T(4,128)} %param.8) | copy-start | bytes 196
  95.7 21.2 %all-to-all-start = ((bf16[2,1,2,2,256,256]{5,4,3,2,1,0:T(8,128)(2,1)}), bf16[2,1,2,2,256,256]{5,4,3,2,1,0:T(8,128)(2,1)S(1)}, u32[]{:S(2)}, u32[]{:S(2)}) async-start(bf16[2,1,2,2,256,256]{5,4,3,2,1,0:T(8,128)(2,1)} %copy.13), calls=%async_computation | async-start | bytes 2097152 | tf_op jit(solution)/shard_map/all_to_all | solution.py:116
where the time goes:
time: 120 us
  blocking collectives  93.1 us (78%)
  matrix products  15.5 us (13%)
  local copies, waits for them, and re-layouts  5.32 us (4%)
  starting transfers between devices  3.89 us (3%)
  other arithmetic  1.86 us (2%)
    psum x1, blocking collectives, local(): whole = lax.psum(partial_value, 'space').astype(jnp.bfloat16)  79.3 us
    all_gather x1, blocking collectives, local(): lax.all_gather(mixed_peramb, 'space', axis=2, tiled=True)  13.8 us
    all_to_all x1, starting transfers between devices, local(): lax.all_to_all(outgoing, 'tm', split_axis=0, concat_axis=0, tiled=True)  3.89 us
    dot_general x4, matrix products, elemental_terms(): lax.dot_general(imag_vec, imag_turned, contract_dims, preferred_element_t...  3.57 us
    convert_element_type x1, local copies, waits for them, and re-layouts, local(): whole = lax.psum(partial_value, 'space').astype(jnp.bfloat16)  2.54 us
  transfers between devices with their start and end apart: 1, of which 0 were waited for; matrix products, arithmetic and copies ran while one was open for 3% of the time, Pallas kernels for 0%

commit v1 on v0

v1 whole, which is shorter than its diff:
```python
import math

import jax
import jax.numpy as jnp
from jax import lax
from jax.experimental import pallas as pl
from jax.experimental.pallas import tpu as pltpu
from jax.sharding import PartitionSpec as P

LAT = 48
NT = (((1,), (1,)), ((), ()))
NN = (((1,), (0,)), ((), ()))


def phases(momenta, site_ids):
    xcoord = (site_ids % LAT).astype(jnp.float32)
    ycoord = (site_ids // LAT % LAT).astype(jnp.float32)
    zcoord = (site_ids // (LAT * LAT)).astype(jnp.float32)
    mom_float = momenta.astype(jnp.float32)
    angles = (
        mom_float[:, 0:1] * xcoord + mom_float[:, 1:2] * ycoord + mom_float[:, 2:3] * zcoord
    ) * (2.0 * math.pi / LAT)
    return (jnp.cos(angles), jnp.sin(angles))


def mm(left, right, dims):
    return lax.dot_general(left, right, dims, preferred_element_type=jnp.float32)


def elemental_kernel(scal, cos_ref, sin_ref, eig_ref, own_ref, *rest):
    sends, acc = rest[:-1], rest[-1]
    moms, rows = own_ref.shape[0], own_ref.shape[2]
    vecs, sites = eig_ref.shape[1:]
    places = len(sends) + 1
    step = pl.program_id(0)

    @pl.when(step == 0)
    def _():
        acc[...] = jnp.zeros_like(acc)

    both = eig_ref[...].reshape(2 * vecs, sites)
    real_wide = eig_ref[0].astype(jnp.float32)
    imag_wide = eig_ref[1].astype(jnp.float32)
    for m in range(moms):
        cosine, sine = cos_ref[m : m + 1, :], sin_ref[m : m + 1, :]
        real_turned = (cosine * real_wide + sine * imag_wide).astype(jnp.bfloat16)
        imag_turned = (cosine * imag_wide - sine * real_wide).astype(jnp.bfloat16)
        by_real = mm(both, real_turned, NT)
        by_imag = mm(both, imag_turned, NT)
        acc[m, 0] += by_real[:vecs] + by_imag[vecs:]
        acc[m, 1] += by_imag[:vecs] - by_real[vecs:]

    @pl.when(step == pl.num_programs(0) - 1)
    def _():
        for d, out in enumerate((own_ref, *sends)):
            first = pl.multiple_of(lax.rem(scal[0] + d, places) * rows, rows)
            out[...] = acc[:, :, pl.ds(first, rows), :].astype(out.dtype)


def partial_elementals(eigvecs, cosine, sine, scal, places):
    _, _, colours, vecs, sites = eigvecs.shape
    moms = cosine.shape[0]
    block = (moms, 2, vecs // places, vecs)
    whole = lambda c, s: (0, 0, 0, 0)
    return pl.pallas_call(
        elemental_kernel,
        grid_spec=pltpu.PrefetchScalarGridSpec(
            num_scalar_prefetch=1,
            grid=(colours,),
            in_specs=[
                pl.BlockSpec((moms, sites), lambda c, s: (0, 0)),
                pl.BlockSpec((moms, sites), lambda c, s: (0, 0)),
                pl.BlockSpec((None, 2, None, vecs, sites), lambda c, s: (s[1], 0, c, 0, 0)),
            ],
            out_specs=[pl.BlockSpec(block, whole)] * places,
            scratch_shapes=[pltpu.VMEM((moms, 2, vecs, vecs), jnp.float32)],
        ),
        out_shape=[jax.ShapeDtypeStruct(block, jnp.float32)]
        + [jax.ShapeDtypeStruct(block, jnp.bfloat16)] * (places - 1),
        name="elementals",
    )(scal, cosine, sine, eigvecs)


def mix_kernel(scal, spin, per_ref, out_ref):
    pairs, _, sinks, sources = per_ref.shape[:4]
    for q in range(pairs):
        for c in range(2):
            total = None
            for a in range(sinks):
                for b in range(sources):
                    term = spin[a, b] * per_ref[q, c, a, b].astype(jnp.float32)
                    total = term if total is None else total + term
            out_ref[q, c] = total.astype(out_ref.dtype)


def mixed_rows(perambulators, spin_weights, scal, parts):
    pairs, _, sinks, sources, rows, vecs = perambulators.shape
    take = rows // parts
    return pl.pallas_call(
        mix_kernel,
        grid_spec=pltpu.PrefetchScalarGridSpec(
            num_scalar_prefetch=1,
            grid=(1,),
            in_specs=[
                pl.BlockSpec(memory_space=pltpu.SMEM),
                pl.BlockSpec(
                    (pairs, 2, sinks, sources, take, vecs), lambda i, s: (0, 0, 0, 0, s[2], 0)
                ),
            ],
            out_specs=pl.BlockSpec((pairs, 2, take, vecs), lambda i, s: (0, 0, 0, 0)),
        ),
        out_shape=jax.ShapeDtypeStruct((pairs, 2, take, vecs), jnp.bfloat16),
        name="mixing",
    )(scal, spin_weights, perambulators)


def product_kernel(places, parts, scal, sink_ref, *rest):
    sources, mixes = rest[:places], rest[places : 2 * places]
    out_ref, source, mixed = rest[2 * places :]
    pairs, moms, _, rows, vecs = sink_ref.shape
    take = rows // parts
    for q in range(pairs):
        for d in range(places):
            place = lax.rem(scal[0] + (places - d), places)
            first = pl.multiple_of(place * rows, rows)
            source[:, :, pl.ds(first, rows), :] = sources[d][q]
            for h in range(parts):
                start = pl.multiple_of(place * rows + h * take, take)
                mixed[:, pl.ds(start, take), :] = mixes[d][h, q]
        for m in range(moms):
            both = sink_ref[q, m].reshape(2 * rows, vecs)
            by_real = mm(both, mixed[0], NN)
            by_imag = mm(both, mixed[1], NN)
            left_real = (by_real[:rows] - by_imag[rows:]).astype(jnp.bfloat16)
            left_imag = (by_imag[:rows] + by_real[rows:]).astype(jnp.bfloat16)
            left = jnp.concatenate([left_real, left_imag], 0)
            on_real = mm(left, source[m, 0], NT)
            on_imag = mm(left, source[m, 1], NT)
            out_ref[q, m, 0] = (on_real[:rows] + on_imag[rows:]).astype(out_ref.dtype)
            out_ref[q, m, 1] = (on_real[rows:] - on_imag[:rows]).astype(out_ref.dtype)


def products(sink, sources, mixes, scal):
    places, parts = len(sources), mixes[0].shape[0]
    pairs, moms, _, rows, vecs = sink.shape
    vmem = pl.BlockSpec(memory_space=pltpu.VMEM)
    return pl.pallas_call(
        lambda *refs: product_kernel(places, parts, *refs),
        in_specs=[pl.BlockSpec(memory_space=pltpu.SMEM)] + [vmem] * (1 + 2 * places),
        out_specs=vmem,
        out_shape=jax.ShapeDtypeStruct(sink.shape, jnp.bfloat16),
        scratch_shapes=[
            pltpu.VMEM((moms, 2, vecs, vecs), jnp.bfloat16),
            pltpu.VMEM((2, vecs, vecs), jnp.bfloat16),
        ],
        name="products",
    )(scal, sink, *sources, *mixes)


def shifted(value, axis, size, by):
    return lax.ppermute(value, axis, [(i, (i + by) % size) for i in range(size)])


def pick(stack, index):
    chosen = stack[0]
    for k in range(1, len(stack)):
        chosen = jnp.where(index == k, stack[k], chosen)
    return chosen


def local(eigvecs, momenta, pairs, spin_weights, perambulators):
    times_dev, sites_dev = eigvecs.shape[0], eigvecs.shape[4]
    pair_dev, rows_dev = perambulators.shape[0], perambulators.shape[4]
    tm_size, space_size, mom_size = (lax.axis_size(n) for n in ("tm", "space", "mom"))
    my_group, my_place = lax.axis_index("tm"), lax.axis_index("space")
    site_ids = my_place * sites_dev + jnp.arange(sites_dev, dtype=jnp.int32)
    cosine, sine = phases(momenta, site_ids)
    parts = mom_size if rows_dev % (16 * mom_size) == 0 else 1

    asked = []
    for d in range(1, tm_size):
        for p in range(pair_dev):
            asked.append(pairs[(my_group + d) % tm_size * pair_dev + p, 1])
    first = jnp.int32(0)
    for time in reversed(asked):
        first = jnp.where(time // times_dev == my_group, time % times_dev, first)

    def slot_of(time):
        return (time % times_dev - first) % times_dev

    half = lax.axis_index("mom") if parts > 1 else jnp.int32(0)
    slots = []
    for k in range(times_dev):
        scal = jnp.stack([my_place, (first + k) % times_dev, half])
        own, *sends = partial_elementals(eigvecs, cosine, sine, scal, space_size)
        total = own
        for d, send in enumerate(sends, 1):
            total = total + shifted(send, "space", space_size, d).astype(jnp.float32)
        slots.append(total.astype(jnp.bfloat16))

    mine = mixed_rows(perambulators, spin_weights, scal, parts)
    mixes = [mine] + [shifted(mine, "space", space_size, d) for d in range(1, space_size)]
    if parts > 1:
        stacked = jnp.stack(mixes)
        held = [stacked] + [shifted(stacked, "mom", parts, d) for d in range(1, parts)]
        halves = [pick(held, (half - h) % parts) for h in range(parts)]
        mixes = [jnp.stack([value[d] for value in halves]) for d in range(space_size)]
    else:
        mixes = [value[None] for value in mixes]

    own_pairs = [pairs[my_group * pair_dev + p] for p in range(pair_dev)]
    few = (tm_size - 1) * pair_dev == 1
    source = jnp.stack([pick(slots, slot_of(pair[1])) for pair in own_pairs])
    for d in range(1, tm_size):
        wanted = asked[(d - 1) * pair_dev : d * pair_dev]
        out = jnp.stack([slots[0] if few else pick(slots, slot_of(time)) for time in wanted])
        arrived = shifted(out, "tm", tm_size, d)
        for p, pair in enumerate(own_pairs):
            here = pair[1] // times_dev == (my_group - d) % tm_size
            source = source.at[p].set(jnp.where(here, arrived[p], source[p]))
    sources = [source] + [shifted(source, "space", space_size, d) for d in range(1, space_size)]
    sink = jnp.stack([pick(slots, slot_of(pair[0])) for pair in own_pairs])
    return products(sink, sources, mixes, scal)


def solution(mesh):
    return jax.shard_map(
        local,
        mesh=mesh,
        in_specs=(
            P(("ens", "tm"), None, None, None, "space"),
            P("mom", None),
            P(),
            P(),
            P(("ens", "tm"), None, None, None, "space", None),
        ),
        out_specs=P(("ens", "tm"), "mom", None, "space", None),
        check_vma=False,
    )
```

time: 120 us -> 66.8 us (0.56)
  blocking collectives: 93.1 us -> 0 us
  starting transfers between devices: 3.89 us -> 21 us
  Pallas kernels: 0 us -> 15.6 us
  matrix products: 15.5 us -> 0 us
  waiting for transfers between devices: 0.01 us -> 11.4 us
  between operations: 0.38 us -> 7.09 us
  other arithmetic: 1.86 us -> 7.06 us
  local copies, waits for them, and re-layouts: 5.32 us -> 4.05 us
    psum x1 -> x0, blocking collectives: 79.3 us -> none  [local(): whole = lax.psum(partial_value, 'space').astype(jnp.bfloat16)]
    ppermute x0 -> x14, starting transfers between devices: none -> 21 us  [shifted(): lax.ppermute(value, axis, [(i, (i + by) % size) for i in range(size)])]
    pallas_call x0 -> x4, Pallas kernels: none -> 15.6 us  [the longest x2 10.8 us: partial_elementals(): pl.pallas_call(elemental_kernel, grid_spec=pltpu.PrefetchScalarGridSpec(n...]
    dot_general x27 -> x0, matrix products: 15.5 us -> none  [the longest x4 3.57 us: elemental_terms(): lax.dot_general(imag_vec, imag_turned, contract_dims, preferred_element_t...]
    all_gather x1 -> x0, blocking collectives: 13.8 us -> none  [local(): lax.all_gather(mixed_peramb, 'space', axis=2, tiled=True)]
    ppermute x0 -> x14, waiting for transfers between devices: none -> 11.4 us  [shifted(): lax.ppermute(value, axis, [(i, (i + by) % size) for i in range(size)])]
    another operation x8, other arithmetic: 0.44 us -> 4.43 us  [the longest x4 2.53 us: local(): jnp.stack([value[d] for value in halves])]
    all_to_all x1 -> x0, starting transfers between devices: 3.89 us -> none  [local(): lax.all_to_all(outgoing, 'tm', split_axis=0, concat_axis=0, tiled=True)]
  transfers between devices with their start and end apart: 1 -> 14, of which waited for: 0 -> 3; matrix products, arithmetic and copies ran while one was open for 3% -> 10% of each run, Pallas kernels for 0% -> 16%
where the time goes in v1:
time: 66.8 us; the launch traced here: 66.2 us
  starting transfers between devices  21 us (31%)
  Pallas kernels  15.6 us (23%)
  waiting for transfers between devices  11.4 us (17%)
  between operations  7.09 us (11%)
  other arithmetic  7.06 us (11%)
  local copies, waits for them, and re-layouts  4.05 us (6%)
    ppermute x14, starting transfers between devices, shifted(): lax.ppermute(value, axis, [(i, (i + by) % size) for i in range(size)])  21 us
    ppermute x14, waiting for transfers between devices, shifted(): lax.ppermute(value, axis, [(i, (i + by) % size) for i in range(size)])  11.4 us
    pallas_call x2, Pallas kernels, partial_elementals(): pl.pallas_call(elemental_kernel, grid_spec=pltpu.PrefetchScalarGridSpec(n...  10.8 us
    another operation x4, other arithmetic, local(): jnp.stack([value[d] for value in halves])  2.53 us
    pallas_call x1, Pallas kernels, mixed_rows(): pl.pallas_call(mix_kernel, grid_spec=pltpu.PrefetchScalarGridSpec(num_sca...  2.43 us
    pallas_call x1, Pallas kernels, products(): pl.pallas_call(lambda *refs: product_kernel(places, parts, *refs), in_spe...  2.41 us
    unnamed x14, local copies, waits for them, and re-layouts  1.98 us
  transfers between devices with their start and end apart: 14, of which 3 were waited for; matrix products, arithmetic and copies ran while one was open for 10% of the time, Pallas kernels for 16%

profile of v1, /device:TPU:0, one launch (start us, length us, event | category | flops | bytes accessed | tf_op | source)
XLA Modules:
  0.0 66.2 jit_solution(4682772097705272812)
XLA Ops:
  0.0 0.7 %copy-done = s32[2,2]{1,0:T(2,128)S(1)} copy-done((s32[2,2]{1,0:T(2,128)S(1)}, s32[2,2]{1,0:T(2,128)}, u32[]{:S(2)}) %copy-start) | copy-done | bytes 40
  0.7 0.6 constant_dynamic-slice_fusion.1
  3.9 0.6 add_add_fusion.scal.refs_0_
  4.5 2.4 %mixing.1 = bf16[1,2,32,256]{3,2,1,0:T(8,128)(2,1)} custom-call(s32[3]{0:T(128)} %add_add_fusion.scal.refs_0_, f32[4,4]{1,0:T(4,128)} %spin.1, bf16[1,2,4,4,64,256]{5,4,3,2,1,0:T(8,128)(2,1)} %per_ref.1), custom_call_target="tpu_custom_call" | custom-call | tf_op jit(solution)/shard_map/mixing/pallas_call | solution.py:99
  6.9 5.1 %collective-permute-start.12 = (bf16[1,2,32,256]{3,2,1,0:T(8,128)(2,1)}, bf16[1,2,32,256]{3,2,1,0:T(8,128)(2,1)S(1)}, u32[]{:S(2)}, u32[]{:S(2)}) collective-permute-start(bf16[1,2,32,256]{3,2,1,0:T(8,128)(2,1)} %mixing.1), channel_id=1, source_target_pairs={{0,12},{4,0},{8,4},{12,8},{1,13},{5,1},{9,5},{13,9},{2,14},{6,2},{... | collective-permute-start | bytes 98312 | tf_op jit(solution)/shard_map/ppermute | solution.py:161
  12.0 1.0 %collective-permute-start.10 = (bf16[1,2,32,256]{3,2,1,0:T(8,128)(2,1)}, bf16[1,2,32,256]{3,2,1,0:T(8,128)(2,1)S(1)}, u32[]{:S(2)}, u32[]{:S(2)}) collective-permute-start(bf16[1,2,32,256]{3,2,1,0:T(8,128)(2,1)} %mixing.1), channel_id=1, source_target_pairs={{0,4},{4,8},{8,12},{12,0},{1,5},{5,9},{9,13},{13,1},{2,6},{6,10},{... | collective-permute-start | bytes 98312 | tf_op jit(solution)/shard_map/ppermute | solution.py:161
  13.1 0.6 add_add_fusion.1.scal
  13.7 0.7 %convert_element_type.48 = f32[2,3]{1,0:T(2,128)S(1)} convert(s32[2,3]{1,0:T(2,128)} %param.8) | non-fusion elementwise | flops 6 | bytes 48 | tf_op jit(solution)/shard_map/convert_element_type | solution.py:19
  14.6 0.7 %fusion.10 = (f32[2,512]{1,0:T(2,128)}, f32[2,512]{1,0:T(2,128)S(1)}) fusion(f32[512]{0:T(512)S(1)} %fusion.7, f32[2]{0:T(128)S(1)} %get-tuple-element.34, f32[512]{0:T(512)S(1)} %get-tuple-element.53, f32[2]{0:T(128)S(1)} %get-tuple-element.35, f32[512]{0:T(512)S(1)} %get-tuple-element.52, f32[2]{0:T(128)S(1)} %get-tuple-element.33), kind=kLoop, calls=%fused_computation.36 | loop fusion | flops 6144 | bytes 14360 | tf_op jit(solution)/shard_map/sin | solution.py:23
  15.3 0.7 %cos.3.cos_ref = f32[2,512]{1,0:T(2,128)} cosine(f32[2,512]{1,0:T(2,128)S(1)} %get-tuple-element.39) | non-fusion elementwise | bytes 8192 | tf_op jit(solution)/shard_map/cos | solution.py:23
  16.0 5.4 %elementals.3 = (f32[2,2,64,256]{3,2,1,0:T(8,128)}, bf16[2,2,64,256]{3,2,1,0:T(8,128)(2,1)}, bf16[2,2,64,256]{3,2,1,0:T(8,128)(2,1)}, bf16[2,2,64,256]{3,2,1,0:T(8,128)(2,1)}) custom-call(s32[3]{0:T(128)} %add_add_fusion.1.scal, f32[2,512]{1,0:T(2,128)} %cos.3.cos_ref, f32[2,512]{1,0:T(2,128)} %get-tuple-element.38.sin_ref, bf16[2,2,3,256,512]{4,3,2,1,0:T(8,128)(2,1)} %eig_ref.3), custom_call_target="tpu_custom_call" | custom-call | tf_op jit(solution)/shard_map/elementals/pallas_call | solution.py:65
  21.4 2.8 %collective-permute-start.5 = (bf16[2,2,64,256]{3,2,1,0:T(8,128)(2,1)}, bf16[2,2,64,256]{3,2,1,0:T(8,128)(2,1)S(1)}, u32[]{:S(2)}, u32[]{:S(2)}) collective-permute-start(bf16[2,2,64,256]{3,2,1,0:T(8,128)(2,1)} %get-tuple-element.32), channel_id=1, source_target_pairs={{0,12},{4,0},{8,4},{12,8},{1,13},{5,1},{9,5},{13,9},{2,14},{6,2},{... | collective-permute-start | bytes 393224 | tf_op jit(solution)/shard_map/ppermute | solution.py:161
  24.2 1.1 %collective-permute-start.4 = (bf16[2,2,64,256]{3,2,1,0:T(8,128)(2,1)}, bf16[2,2,64,256]{3,2,1,0:T(8,128)(2,1)S(1)}, u32[]{:S(2)}, u32[]{:S(2)}) collective-permute-start(bf16[2,2,64,256]{3,2,1,0:T(8,128)(2,1)} %get-tuple-element.31), channel_id=1, source_target_pairs={{0,8},{4,12},{8,0},{12,4},{1,9},{5,13},{9,1},{13,5},{2,10},{6,14},... | collective-permute-start | bytes 393224 | tf_op jit(solution)/shard_map/ppermute | solution.py:161
  25.4 0.6 fusion.13
  28.6 5.3 %elementals.2 = (f32[2,2,64,256]{3,2,1,0:T(8,128)}, bf16[2,2,64,256]{3,2,1,0:T(8,128)(2,1)}, bf16[2,2,64,256]{3,2,1,0:T(8,128)(2,1)}, bf16[2,2,64,256]{3,2,1,0:T(8,128)(2,1)}) custom-call(s32[3]{0:T(128)} %add_add_fusion.scal.refs_0_, f32[2,512]{1,0:T(2,128)} %cos.3.cos_ref, f32[2,512]{1,0:T(2,128)} %get-tuple-element.38.sin_ref, ...), custom_call_target="tpu_custom_call" | custom-call | tf_op jit(solution)/shard_map/elementals/pallas_call | solution.py:65
  35.7 3.9 %collective-permute-start.2 = (bf16[2,2,64,256]{3,2,1,0:T(8,128)(2,1)}, bf16[2,2,64,256]{3,2,1,0:T(8,128)(2,1)S(1)}, u32[]{:S(2)}, u32[]{:S(2)}) collective-permute-start(bf16[2,2,64,256]{3,2,1,0:T(8,128)(2,1)} %get-tuple-element.28), channel_id=1, source_target_pairs={{0,12},{4,0},{8,4},{12,8},{1,13},{5,1},{9,5},{13,9},{2,14},{6,2},{... | collective-permute-start | bytes 393224 | tf_op jit(solution)/shard_map/ppermute | solution.py:161
  39.6 0.7 %collective-permute-start = (bf16[2,2,64,256]{3,2,1,0:T(8,128)(2,1)}, bf16[2,2,64,256]{3,2,1,0:T(8,128)(2,1)S(1)}, u32[]{:S(2)}, u32[]{:S(2)}) collective-permute-start(bf16[2,2,64,256]{3,2,1,0:T(8,128)(2,1)} %get-tuple-element.26), channel_id=1, source_target_pairs={{0,4},{4,8},{8,12},{12,0},{1,5},{5,9},{9,13},{13,1},{2,6},{6,10},{... | collective-permute-start | bytes 393224 | tf_op jit(solution)/shard_map/ppermute | solution.py:161
  40.4 1.6 %collective-permute-start.6 = (bf16[1,2,2,64,256]{4,3,2,1,0:T(8,128)(2,1)S(1)}, bf16[1,2,2,64,256]{4,3,2,1,0:T(8,128)(2,1)S(1)}, u32[]{:S(2)}, u32[]{:S(2)}) collective-permute-start(bf16[1,2,2,64,256]{4,3,2,1,0:T(8,128)(2,1)S(1)} %bitcast.20), channel_id=1, source_target_pairs={{0,2},{2,0},{1,3},{3,1},{4,6},{6,4},{5,7},{7,5},{8,10},{10,8},{9,1... | collective-permute-start | bytes 393224 | tf_op jit(solution)/shard_map/ppermute | solution.py:161
  42.0 0.6 pad_maximum_fusion.1.refs_6_
  42.6 0.6 pad_maximum_fusion.2.refs_7_
  43.3 0.6 pad_maximum_fusion.3.refs_8_
  43.9 0.6 pad_maximum_fusion.4.refs_9_
  44.5 5.5 %collective-permute-done.1 = bf16[2,2,64,256]{3,2,1,0:T(8,128)(2,1)S(1)} collective-permute-done((bf16[2,2,64,256]{3,2,1,0:T(8,128)(2,1)}, bf16[2,2,64,256]{3,2,1,0:T(8,128)(2,1)S(1)}, u32[]{:S(2)}, u32[]{:S(2)}) %collective-permute-start.1) | collective-permute-done | bytes 131104 | tf_op jit(solution)/shard_map/ppermute | solution.py:161
  50.0 1.1 %fusion = (bf16[1,2,2,64,256]{4,3,2,1,0:T(8,128)(2,1)S(1)}, bf16[2,2,64,256]{3,2,1,0:T(8,128)(2,1)S(1)}) fusion(bf16[1,2,2,64,256]{4,3,2,1,0:T(8,128)(2,1)S(1)} %collective-permute-done.6, bf16[2,2,64,256]{3,2,1,0:T(8,128)(2,1)S(1)} %add_convert_fusion, pred[]{:T(512)S(6)} %eq.36, pred[]{:T(512)S(6)} %eq.35, ...), kind=kLoop, calls=%fused_computation.4 | loop fusion | flops 589824 | bytes 1179650 | tf_op jit(solution)/shard_map/scatter | solution.py:220
  51.2 1.9 %collective-permute-start.8 = (bf16[1,2,2,64,256]{4,3,2,1,0:T(8,128)(2,1)S(1)}, bf16[1,2,2,64,256]{4,3,2,1,0:T(8,128)(2,1)S(1)}, u32[]{:S(2)}, u32[]{:S(2)}) collective-permute-start(bf16[1,2,2,64,256]{4,3,2,1,0:T(8,128)(2,1)S(1)} %get-tuple-element.36.refs_2_), channel_id=1, source_target_pairs={{0,8},{4,12},{8,0},{12,4},{1,9},{5,13},{9,1},{13,5},{2,10},{6,14},... | collective-permute-start | bytes 393224 | tf_op jit(solution)/shard_map/ppermute | solution.py:161
  53.1 2.8 %collective-permute-start.9 = (bf16[1,2,2,64,256]{4,3,2,1,0:T(8,128)(2,1)S(1)}, bf16[1,2,2,64,256]{4,3,2,1,0:T(8,128)(2,1)S(1)}, u32[]{:S(2)}, u32[]{:S(2)}) collective-permute-start(bf16[1,2,2,64,256]{4,3,2,1,0:T(8,128)(2,1)S(1)} %get-tuple-element.36.refs_2_), channel_id=1, source_target_pairs={{0,12},{4,0},{8,4},{12,8},{1,13},{5,1},{9,5},{13,9},{2,14},{6,2},{... | collective-permute-start | bytes 393224 | tf_op jit(solution)/shard_map/ppermute | solution.py:161
  55.9 0.7 %select_bitcast_fusion.refs_1_ = bf16[1,2,2,64,256]{4,3,2,1,0:T(8,128)(2,1)} fusion(bf16[2,2,64,256]{3,2,1,0:T(8,128)(2,1)S(1)} %get-tuple-element.37, bf16[2,2,64,256]{3,2,1,0:T(8,128)(2,1)S(1)} %add_convert_fusion, pred[]{:T(512)S(6)} %eq.34), kind=kLoop, calls=%fused_computation.5 | loop fusion | flops 65536 | bytes 393217 | tf_op jit(solution)/shard_map/stack | solution.py:222
  56.6 2.8 %collective-permute-done.7.refs_3_ = bf16[1,2,2,64,256]{4,3,2,1,0:T(8,128)(2,1)S(1)} collective-permute-done((bf16[1,2,2,64,256]{4,3,2,1,0:T(8,128)(2,1)S(1)}, bf16[1,2,2,64,256]{4,3,2,1,0:T(8,128)(2,1)S(1)}, u32[]{:S(2)}, u32[]{:S(2)}) %collective-permute-start.7) | collective-permute-done | bytes 131104 | tf_op jit(solution)/shard_map/ppermute | solution.py:161
  59.4 3.1 %collective-permute-done.8.refs_4_ = bf16[1,2,2,64,256]{4,3,2,1,0:T(8,128)(2,1)S(1)} collective-permute-done((bf16[1,2,2,64,256]{4,3,2,1,0:T(8,128)(2,1)S(1)}, bf16[1,2,2,64,256]{4,3,2,1,0:T(8,128)(2,1)S(1)}, u32[]{:S(2)}, u32[]{:S(2)}) %collective-permute-start.8) | collective-permute-done | bytes 131104 | tf_op jit(solution)/shard_map/ppermute | solution.py:161
  62.5 0.6 copy-done.5
  63.2 0.7 copy-done.6
  63.8 2.4 %products.1 = bf16[1,2,2,64,256]{4,3,2,1,0:T(8,128)(2,1)} custom-call(s32[3]{0:T(128)} %add_add_fusion.scal.refs_0_, bf16[1,2,2,64,256]{4,3,2,1,0:T(8,128)(2,1)} %select_bitcast_fusion.refs_1_, bf16[1,2,2,64,256]{4,3,2,1,0:T(8,128)(2,1)} %copy-done.1, bf16[1,2,2,64,256]{4,3,2,1,0:T(8,128)(2,1)} %copy-done.4, bf16[1,2,2,64,256]{4,3,2,1,0:T(8,128)(2,1)} %copy-done.5, ...), custom_call_target="tpu_custom_call" | custom-call | tf_op jit(solution)/shard_map/products/pallas_call | solution.py:147
  (35 shorter events, 0.6 us)
Async XLA Ops:
  0.0 0.7 %copy-start = (s32[2,2]{1,0:T(2,128)S(1)}, s32[2,2]{1,0:T(2,128)}, u32[]{:S(2)}) copy-start(s32[2,2]{1,0:T(2,128)} %param.9) | copy-start | bytes 52
  6.9 18.4 %collective-permute-start.12 = (bf16[1,2,32,256]{3,2,1,0:T(8,128)(2,1)}, bf16[1,2,32,256]{3,2,1,0:T(8,128)(2,1)S(1)}, u32[]{:S(2)}, u32[]{:S(2)}) collective-permute-start(bf16[1,2,32,256]{3,2,1,0:T(8,128)(2,1)} %mixing.1), channel_id=1, source_target_pairs={{0,12},{4,0},{8,4},{12,8},{1,13},{5,1},{9,5},{13,9},{2,14},{6,2},{... | collective-permute-start | bytes 98312 | tf_op jit(solution)/shard_map/ppermute | solution.py:161
  12.0 23.7 %collective-permute-start.11 = (bf16[1,2,32,256]{3,2,1,0:T(8,128)(2,1)}, bf16[1,2,32,256]{3,2,1,0:T(8,128)(2,1)S(1)}, u32[]{:S(2)}, u32[]{:S(2)}) collective-permute-start(bf16[1,2,32,256]{3,2,1,0:T(8,128)(2,1)} %mixing.1), channel_id=1, source_target_pairs={{0,8},{4,12},{8,0},{12,4},{1,9},{5,13},{9,1},{13,5},{2,10},{6,14},... | collective-permute-start | bytes 98312 | tf_op jit(solution)/shard_map/ppermute | solution.py:161
  12.0 27.5 %collective-permute-start.10 = (bf16[1,2,32,256]{3,2,1,0:T(8,128)(2,1)}, bf16[1,2,32,256]{3,2,1,0:T(8,128)(2,1)S(1)}, u32[]{:S(2)}, u32[]{:S(2)}) collective-permute-start(bf16[1,2,32,256]{3,2,1,0:T(8,128)(2,1)} %mixing.1), channel_id=1, source_target_pairs={{0,4},{4,8},{8,12},{12,0},{1,5},{5,9},{9,13},{13,1},{2,6},{6,10},{... | collective-permute-start | bytes 98312 | tf_op jit(solution)/shard_map/ppermute | solution.py:161
  16.0 23.6 %copy-start.2 = (bf16[1,2,32,256]{3,2,1,0:T(8,128)(2,1)S(1)}, bf16[1,2,32,256]{3,2,1,0:T(8,128)(2,1)}, u32[]{:S(2)}) copy-start(bf16[1,2,32,256]{3,2,1,0:T(8,128)(2,1)} %mixing.1) | copy-start | bytes 98308
  21.4 18.9 %copy-start.3 = (f32[2,2,64,256]{3,2,1,0:T(8,128)S(1)}, f32[2,2,64,256]{3,2,1,0:T(8,128)}, u32[]{:S(2)}) copy-start(f32[2,2,64,256]{3,2,1,0:T(8,128)} %get-tuple-element.29) | copy-start | bytes 786436
  21.4 18.2 %collective-permute-start.5 = (bf16[2,2,64,256]{3,2,1,0:T(8,128)(2,1)}, bf16[2,2,64,256]{3,2,1,0:T(8,128)(2,1)S(1)}, u32[]{:S(2)}, u32[]{:S(2)}) collective-permute-start(bf16[2,2,64,256]{3,2,1,0:T(8,128)(2,1)} %get-tuple-element.32), channel_id=1, source_target_pairs={{0,12},{4,0},{8,4},{12,8},{1,13},{5,1},{9,5},{13,9},{2,14},{6,2},{... | collective-permute-start | bytes 393224 | tf_op jit(solution)/shard_map/ppermute | solution.py:161
  24.2 16.1 %collective-permute-start.4 = (bf16[2,2,64,256]{3,2,1,0:T(8,128)(2,1)}, bf16[2,2,64,256]{3,2,1,0:T(8,128)(2,1)S(1)}, u32[]{:S(2)}, u32[]{:S(2)}) collective-permute-start(bf16[2,2,64,256]{3,2,1,0:T(8,128)(2,1)} %get-tuple-element.31), channel_id=1, source_target_pairs={{0,8},{4,12},{8,0},{12,4},{1,9},{5,13},{9,1},{13,5},{2,10},{6,14},... | collective-permute-start | bytes 393224 | tf_op jit(solution)/shard_map/ppermute | solution.py:161
  25.3 15.0 %collective-permute-start.3 = (bf16[2,2,64,256]{3,2,1,0:T(8,128)(2,1)}, bf16[2,2,64,256]{3,2,1,0:T(8,128)(2,1)S(1)}, u32[]{:S(2)}, u32[]{:S(2)}) collective-permute-start(bf16[2,2,64,256]{3,2,1,0:T(8,128)(2,1)} %get-tuple-element.30), channel_id=1, source_target_pairs={{0,4},{4,8},{8,12},{12,0},{1,5},{5,9},{9,13},{13,1},{2,6},{6,10},{... | collective-permute-start | bytes 393224 | tf_op jit(solution)/shard_map/ppermute | solution.py:161
  35.7 8.8 %collective-permute-start.2 = (bf16[2,2,64,256]{3,2,1,0:T(8,128)(2,1)}, bf16[2,2,64,256]{3,2,1,0:T(8,128)(2,1)S(1)}, u32[]{:S(2)}, u32[]{:S(2)}) collective-permute-start(bf16[2,2,64,256]{3,2,1,0:T(8,128)(2,1)} %get-tuple-element.28), channel_id=1, source_target_pairs={{0,12},{4,0},{8,4},{12,8},{1,13},{5,1},{9,5},{13,9},{2,14},{6,2},{... | collective-permute-start | bytes 393224 | tf_op jit(solution)/shard_map/ppermute | solution.py:161
  39.5 10.5 %collective-permute-start.1 = (bf16[2,2,64,256]{3,2,1,0:T(8,128)(2,1)}, bf16[2,2,64,256]{3,2,1,0:T(8,128)(2,1)S(1)}, u32[]{:S(2)}, u32[]{:S(2)}) collective-permute-start(bf16[2,2,64,256]{3,2,1,0:T(8,128)(2,1)} %get-tuple-element.27), channel_id=1, source_target_pairs={{0,8},{4,12},{8,0},{12,4},{1,9},{5,13},{9,1},{13,5},{2,10},{6,14},... | collective-permute-start | bytes 393224 | tf_op jit(solution)/shard_map/ppermute | solution.py:161
  39.6 10.4 %collective-permute-start = (bf16[2,2,64,256]{3,2,1,0:T(8,128)(2,1)}, bf16[2,2,64,256]{3,2,1,0:T(8,128)(2,1)S(1)}, u32[]{:S(2)}, u32[]{:S(2)}) collective-permute-start(bf16[2,2,64,256]{3,2,1,0:T(8,128)(2,1)} %get-tuple-element.26), channel_id=1, source_target_pairs={{0,4},{4,8},{8,12},{12,0},{1,5},{5,9},{9,13},{13,1},{2,6},{6,10},{... | collective-permute-start | bytes 393224 | tf_op jit(solution)/shard_map/ppermute | solution.py:161
  40.3 1.6 %collective-permute-start.13 = (bf16[4,1,2,32,256]{4,3,2,1,0:T(8,128)(2,1)S(1)}, bf16[4,1,2,32,256]{4,3,2,1,0:T(8,128)(2,1)S(1)}, u32[]{:S(2)}, u32[]{:S(2)}) collective-permute-start(bf16[4,1,2,32,256]{4,3,2,1,0:T(8,128)(2,1)S(1)} %pad_maximum_fusion), channel_id=1, source_target_pairs={{0,1},{1,0},{2,3},{3,2},{4,5},{5,4},{6,7},{7,6},{8,9},{9,8},{10,11... | collective-permute-start | bytes 393224 | tf_op jit(solution)/shard_map/ppermute | solution.py:161
  40.4 9.6 %collective-permute-start.6 = (bf16[1,2,2,64,256]{4,3,2,1,0:T(8,128)(2,1)S(1)}, bf16[1,2,2,64,256]{4,3,2,1,0:T(8,128)(2,1)S(1)}, u32[]{:S(2)}, u32[]{:S(2)}) collective-permute-start(bf16[1,2,2,64,256]{4,3,2,1,0:T(8,128)(2,1)S(1)} %bitcast.20), channel_id=1, source_target_pairs={{0,2},{2,0},{1,3},{3,1},{4,6},{6,4},{5,7},{7,5},{8,10},{10,8},{9,1... | collective-permute-start | bytes 393224 | tf_op jit(solution)/shard_map/ppermute | solution.py:161
  51.1 11.4 %copy-start.1 = (bf16[1,2,2,64,256]{4,3,2,1,0:T(8,128)(2,1)}, bf16[1,2,2,64,256]{4,3,2,1,0:T(8,128)(2,1)S(1)}, u32[]{:S(2)}) copy-start(bf16[1,2,2,64,256]{4,3,2,1,0:T(8,128)(2,1)S(1)} %get-tuple-element.36.refs_2_) | copy-start | bytes 393220
  51.1 8.3 %collective-permute-start.7 = (bf16[1,2,2,64,256]{4,3,2,1,0:T(8,128)(2,1)S(1)}, bf16[1,2,2,64,256]{4,3,2,1,0:T(8,128)(2,1)S(1)}, u32[]{:S(2)}, u32[]{:S(2)}) collective-permute-start(bf16[1,2,2,64,256]{4,3,2,1,0:T(8,128)(2,1)S(1)} %get-tuple-element.36.refs_2_), channel_id=1, source_target_pairs={{0,4},{4,8},{8,12},{12,0},{1,5},{5,9},{9,13},{13,1},{2,6},{6,10},{... | collective-permute-start | bytes 393224 | tf_op jit(solution)/shard_map/ppermute | solution.py:161
  51.2 11.3 %collective-permute-start.8 = (bf16[1,2,2,64,256]{4,3,2,1,0:T(8,128)(2,1)S(1)}, bf16[1,2,2,64,256]{4,3,2,1,0:T(8,128)(2,1)S(1)}, u32[]{:S(2)}, u32[]{:S(2)}) collective-permute-start(bf16[1,2,2,64,256]{4,3,2,1,0:T(8,128)(2,1)S(1)} %get-tuple-element.36.refs_2_), channel_id=1, source_target_pairs={{0,8},{4,12},{8,0},{12,4},{1,9},{5,13},{9,1},{13,5},{2,10},{6,14},... | collective-permute-start | bytes 393224 | tf_op jit(solution)/shard_map/ppermute | solution.py:161
  53.1 9.5 %collective-permute-start.9 = (bf16[1,2,2,64,256]{4,3,2,1,0:T(8,128)(2,1)S(1)}, bf16[1,2,2,64,256]{4,3,2,1,0:T(8,128)(2,1)S(1)}, u32[]{:S(2)}, u32[]{:S(2)}) collective-permute-start(bf16[1,2,2,64,256]{4,3,2,1,0:T(8,128)(2,1)S(1)} %get-tuple-element.36.refs_2_), channel_id=1, source_target_pairs={{0,12},{4,0},{8,4},{12,8},{1,13},{5,1},{9,5},{13,9},{2,14},{6,2},{... | collective-permute-start | bytes 393224 | tf_op jit(solution)/shard_map/ppermute | solution.py:161
  59.4 3.1 %copy-start.4 = (bf16[1,2,2,64,256]{4,3,2,1,0:T(8,128)(2,1)}, bf16[1,2,2,64,256]{4,3,2,1,0:T(8,128)(2,1)S(1)}, u32[]{:S(2)}) copy-start(bf16[1,2,2,64,256]{4,3,2,1,0:T(8,128)(2,1)S(1)} %collective-permute-done.7.refs_3_) | copy-start | bytes 393220
  62.5 0.6 copy-start.5
  63.2 0.7 copy-start.6

commit v2 on v0

v2 whole, which is shorter than its diff:
```python
import math

import jax
import jax.numpy as jnp
from jax import lax
from jax.experimental import pallas as pl
from jax.experimental.pallas import tpu as pltpu
from jax.sharding import PartitionSpec as P

LAT = 48
DIRECT = 4
NT = (((1,), (1,)), ((), ()))
NN = (((1,), (0,)), ((), ()))
SMEM = pl.BlockSpec(memory_space=pltpu.SMEM)
VMEM = pl.BlockSpec(memory_space=pltpu.VMEM)
ANY = pl.BlockSpec(memory_space=pl.ANY)
HBM = pl.BlockSpec(memory_space=pltpu.HBM)
LARGE = pltpu.CompilerParams(vmem_limit_bytes=16 * 2**20)
SMALL = pltpu.CompilerParams(vmem_limit_bytes=8 * 2**20)


def mm(left, right, dims):
    return lax.dot_general(left, right, dims, preferred_element_type=jnp.float32)


def asked_times(pairs, tm_size, pair_dev):
    group = lax.axis_index("tm")
    return [
        pairs[lax.rem(group + d, tm_size) * pair_dev + p, 1]
        for d in range(1, tm_size)
        for p in range(pair_dev)
    ]


def first_time(asked, times_dev):
    group = lax.axis_index("tm")
    first = jnp.int32(0)
    for time in reversed(asked):
        first = jnp.where(lax.div(time, times_dev) == group, lax.rem(time, times_dev), first)
    return first


def slot_of(time, first, times_dev):
    return lax.rem(lax.rem(time, times_dev) - first + times_dev, times_dev)


def phases(momenta, moms, first_site, sites):
    site = first_site + lax.broadcasted_iota(jnp.int32, (1, sites), 1)
    xcoord = (site % LAT).astype(jnp.float32)
    ycoord = (site // LAT % LAT).astype(jnp.float32)
    zcoord = (site // (LAT * LAT)).astype(jnp.float32)
    found = []
    for m in range(moms):
        px, py, pz = (momenta[m, k].astype(jnp.float32) for k in range(3))
        angles = (px * xcoord + py * ycoord + pz * zcoord) * (2.0 * math.pi / LAT)
        found.append((jnp.cos(angles), jnp.sin(angles)))
    return found


def mix(spin, per, out):
    for q in range(per.shape[0]):
        for c in range(2):
            total = None
            for a in range(per.shape[2]):
                for b in range(per.shape[3]):
                    term = spin[a, b] * per[q, c, a, b].astype(jnp.float32)
                    total = term if total is None else total + term
            out[q, c] = total.astype(out.dtype)


def elemental_kernel(slot, tm_size, places, direct, parts, pair_dev, momenta, pairs, *refs):
    mixing = parts > 0
    n_outs = places if direct else 2
    if mixing:
        spin, eig, per, mixed, *refs = refs
    else:
        eig, *refs = refs
    outs, (held, acc, sems, *more) = refs[:n_outs], refs[n_outs:]
    times, _, colours, vecs, sites = eig.shape
    moms, rows = outs[0].shape[-4], outs[0].shape[-2]
    place = lax.axis_index("space")
    first = first_time(asked_times(pairs, tm_size, pair_dev), times)
    time = lax.rem(first + slot, times)
    copies = [
        pltpu.make_async_copy(eig.at[time, :, c], held.at[c], sems.at[c]) for c in range(colours)
    ]
    for copy in copies:
        copy.start()
    if mixing:
        per_held, per_sem = more
        take = per_held.shape[4]
        start = 0 if parts == 1 else pl.multiple_of(lax.axis_index("mom") * take, take)
        per_copy = pltpu.make_async_copy(
            per.at[:, :, :, :, pl.ds(start, take), :], per_held, per_sem
        )
        per_copy.start()
    turns = phases(momenta, moms, place * sites, sites)
    for c in range(colours):
        copies[c].wait()
        both = held[c].reshape(2 * vecs, sites)
        real_wide = held[c, 0].astype(jnp.float32)
        imag_wide = held[c, 1].astype(jnp.float32)
        for m, (cosine, sine) in enumerate(turns):
            real_turned = (cosine * real_wide + sine * imag_wide).astype(jnp.bfloat16)
            imag_turned = (cosine * imag_wide - sine * real_wide).astype(jnp.bfloat16)
            by_real = mm(both, real_turned, NT)
            by_imag = mm(both, imag_turned, NT)
            real_part = by_real[:vecs] + by_imag[vecs:]
            imag_part = by_imag[:vecs] - by_real[vecs:]
            if c == 0:
                acc[m, 0] = real_part
                acc[m, 1] = imag_part
            else:
                acc[m, 0] += real_part
                acc[m, 1] += imag_part
    if mixing:
        per_copy.wait()
        mix(spin, per_held, mixed)
    for d in range(places):
        out = outs[d] if direct else outs[d % 2].at[d // 2]
        row = pl.multiple_of((place ^ d) * rows, rows)
        out[...] = acc[:, :, pl.ds(row, rows), :].astype(out.dtype)


def partial_elementals(
    slot, momenta, pairs, eigvecs, tm_size, places, direct, pair_dev, mixing=None
):
    _, _, colours, vecs, sites = eigvecs.shape
    block = (momenta.shape[0], 2, vecs // places, vecs)
    if direct:
        shapes = [jax.ShapeDtypeStruct(block, jnp.float32)]
        shapes += [jax.ShapeDtypeStruct(block, jnp.bfloat16)] * (places - 1)
    else:
        shapes = [
            jax.ShapeDtypeStruct((places // 2, *block), dtype) for dtype in (jnp.float32, jnp.bfloat16)
        ]
    scratch = [
        pltpu.VMEM((colours, 2, vecs, sites), jnp.bfloat16),
        pltpu.VMEM((block[0], 2, vecs, vecs), jnp.float32),
        pltpu.SemaphoreType.DMA((colours,)),
    ]
    ins, operands, parts = [SMEM, SMEM, HBM], (momenta, pairs, eigvecs), 0
    if mixing is not None:
        spin_weights, perambulators, parts = mixing
        count, _, sinks, sources, rows, _ = perambulators.shape
        ins = [SMEM, SMEM, SMEM, HBM, HBM]
        operands = (momenta, pairs, spin_weights, eigvecs, perambulators)
        shapes.insert(0, jax.ShapeDtypeStruct((count, 2, rows // parts, vecs), jnp.bfloat16))
        scratch.append(
            pltpu.VMEM((count, 2, sinks, sources, rows // parts, vecs), jnp.bfloat16)
        )
        scratch.append(pltpu.SemaphoreType.DMA)
    return pl.pallas_call(
        lambda *refs: elemental_kernel(slot, tm_size, places, direct, parts, pair_dev, *refs),
        in_specs=ins,
        out_specs=[VMEM] * len(shapes),
        out_shape=shapes,
        scratch_shapes=scratch,
        compiler_params=LARGE if parts else None,
        name="elementals_mixing" if parts else "elementals",
    )(*operands)


def added(terms):
    total = terms[0][...]
    for term in terms[1:]:
        total = total + term[...].astype(jnp.float32)
    return total.astype(jnp.bfloat16)


def source_kernel(tm_size, times, pair_dev, n_slots, pairs, *refs):
    slots, arrived, out_ref = refs[:n_slots], refs[n_slots:-1], refs[-1]
    group = lax.axis_index("tm")
    first = first_time(asked_times(pairs, tm_size, pair_dev), times)
    for p in range(pair_dev):
        source = pairs[group * pair_dev + p, 1]
        owner, slot = lax.div(source, times), slot_of(source, first, times)
        for k in range(n_slots):
            here = slot == k if n_slots > 1 else True

            @pl.when((owner == group) & here)
            def _(k=k, p=p):
                out_ref[p] = slots[k][...]

        for d in range(1, tm_size):

            @pl.when(owner == lax.rem(group + tm_size - d, tm_size))
            def _(d=d, p=p):
                out_ref[p] = arrived[d - 1][p]


def choose_source(pairs, slots, arrived, tm_size, times, pair_dev):
    return pl.pallas_call(
        lambda *refs: source_kernel(tm_size, times, pair_dev, len(slots), *refs),
        in_specs=[SMEM] + [VMEM] * (len(slots) + len(arrived)),
        out_specs=VMEM,
        out_shape=jax.ShapeDtypeStruct((pair_dev, *slots[0].shape), jnp.bfloat16),
        compiler_params=SMALL,
        name="choose_source",
    )(pairs, *slots, *arrived)


def left_kernel(order, tm_size, times, n_mixes, pairs, *refs):
    mixes, ready = refs[:n_mixes], refs[n_mixes : n_mixes + times - 1]
    terms = refs[n_mixes + times - 1 : -3]
    out_ref, sink_ref, mixed = refs[-3:]
    pair_dev, moms, _, rows, vecs = out_ref.shape
    take = rows // n_mixes
    for e, pieces in enumerate(mixes):
        half = lax.rem(lax.axis_index("mom") + (n_mixes - e), n_mixes) if n_mixes > 1 else 0
        for n, d in enumerate(order):
            start = pl.multiple_of((lax.axis_index("space") ^ d) * rows + half * take, take)
            mixed[:, :, pl.ds(start, take), :] = pieces[n]
    first = first_time(asked_times(pairs, tm_size, pair_dev), times)
    for q in range(pair_dev):
        slot = slot_of(pairs[lax.axis_index("tm") * pair_dev + q, 0], first, times)
        sink_ref[...] = added(terms)
        for k in range(times - 1):

            @pl.when(slot == k)
            def _(k=k):
                sink_ref[...] = ready[k][...]

        for m in range(moms):
            both = sink_ref[m].reshape(2 * rows, vecs)
            by_real = mm(both, mixed[q, 0], NN)
            by_imag = mm(both, mixed[q, 1], NN)
            out_ref[q, m, 0] = (by_real[:rows] - by_imag[rows:]).astype(out_ref.dtype)
            out_ref[q, m, 1] = (by_imag[:rows] + by_real[rows:]).astype(out_ref.dtype)


def left_products(pairs, ready, terms, mixes, order, tm_size, pair_dev):
    block = terms[0].shape
    vecs = block[-1]
    return pl.pallas_call(
        lambda *refs: left_kernel(order, tm_size, len(ready) + 1, len(mixes), *refs),
        in_specs=[SMEM] + [VMEM] * (len(mixes) + len(ready) + len(terms)),
        out_specs=VMEM,
        out_shape=jax.ShapeDtypeStruct((pair_dev, *block), jnp.bfloat16),
        scratch_shapes=[
            pltpu.VMEM(block, jnp.bfloat16),
            pltpu.VMEM((pair_dev, 2, vecs, vecs), jnp.bfloat16),
        ],
        compiler_params=SMALL,
        name="left_products",
    )(pairs, *mixes, *ready, *terms)


def right_kernel(left_ref, *refs):
    sources, (out_ref, whole) = refs[:-2], refs[-2:]
    pairs, moms, _, rows, vecs = left_ref.shape
    for d, source in enumerate(sources):
        start = pl.multiple_of((lax.axis_index("space") ^ d) * rows, rows)
        whole[:, :, :, pl.ds(start, rows), :] = source[...]
    for q in range(pairs):
        for m in range(moms):
            left = left_ref[q, m].reshape(2 * rows, vecs)
            on_real = mm(left, whole[q, m, 0], NT)
            on_imag = mm(left, whole[q, m, 1], NT)
            out_ref[q, m, 0] = (on_real[:rows] + on_imag[rows:]).astype(out_ref.dtype)
            out_ref[q, m, 1] = (on_real[rows:] - on_imag[:rows]).astype(out_ref.dtype)


def right_products(left, sources):
    pairs, moms, _, _, vecs = left.shape
    return pl.pallas_call(
        right_kernel,
        in_specs=[VMEM] * (1 + len(sources)),
        out_specs=VMEM,
        out_shape=jax.ShapeDtypeStruct(left.shape, jnp.bfloat16),
        scratch_shapes=[pltpu.VMEM((pairs, moms, 2, vecs, vecs), jnp.bfloat16)],
        compiler_params=SMALL,
        name="right_products",
    )(left, *sources)


def swapped(value, places, by):
    return lax.ppermute(value, "space", [(i, i ^ by) for i in range(places)])


def shifted(value, axis, size, by):
    return lax.ppermute(value, axis, [(i, (i + by) % size) for i in range(size)])


def sum_of(terms):
    total = terms[0]
    for term in terms[1:]:
        total = total + term.astype(jnp.float32)
    return total.astype(jnp.bfloat16)


def pick(stack, index):
    chosen = stack[0]
    for k in range(1, len(stack)):
        chosen = jnp.where(index == k, stack[k], chosen)
    return chosen


def local(eigvecs, momenta, pairs, spin_weights, perambulators):
    times_dev = eigvecs.shape[0]
    pair_dev, rows_dev = perambulators.shape[0], perambulators.shape[4]
    tm_size, places, mom_size = (lax.axis_size(n) for n in ("tm", "space", "mom"))
    parts = mom_size if rows_dev % (16 * mom_size) == 0 else 1

    few = (tm_size - 1) * pair_dev == 1 and times_dev == 2
    owners = pairs[:, 1] // times_dev
    late = (owners[0] == owners[1]) & (pairs[0, 1] != pairs[1, 1])
    terms, late_pairs = [], pairs
    for k in range(times_dev):
        last = k == times_dev - 1
        direct = k == 0 and places <= DIRECT
        blocks = partial_elementals(
            k, momenta, late_pairs, eigvecs, tm_size, places, direct, pair_dev,
            (spin_weights, perambulators, parts) if last else None,
        )
        late_pairs, blocks = lax.optimization_barrier((pairs, blocks))
        if last:
            mine, *blocks = blocks
        if direct:
            own, *sends = blocks
            terms.append([own] + [swapped(s, places, d) for d, s in enumerate(sends, 1)])
        else:
            kept, sent = blocks
            by = 1
            received = swapped(sent, places, by)
            while kept.shape[0] > 1:
                total = kept + received.astype(jnp.float32)
                kept, sent, by = total[0::2], total[1::2].astype(jnp.bfloat16), by * 2
                received = swapped(sent, places, by)
            terms.append([kept[0], received[0]])
    ready = [sum_of(parts_of) for parts_of in terms[:-1]]

    mixes, order, by = mine[None], [0], places // 2
    while by:
        mixes = jnp.concatenate([mixes, swapped(mixes, places, by)])
        order += [d ^ by for d in order]
        by //= 2
    mixes = [mixes] + [shifted(mixes, "mom", parts, e) for e in range(1, parts)]

    def gather(source):
        there = {d: swapped(source, places, d) for d in sorted(range(1, places), key=lambda d: -(d ^ 1))}
        return [source] + [there[d] for d in range(1, places)]

    left = left_products(pairs, ready, terms[-1], mixes, order, tm_size, pair_dev)
    if few:
        arrived = [shifted(ready[0][None], "tm", tm_size, 1)]
        sources = gather(choose_source(pairs, ready, arrived, tm_size, times_dev, pair_dev))
        return lax.cond(
            late,
            lambda left, final, *sources: right_products(left, gather(late_source(pairs, sources[0], final, times_dev))),
            lambda left, final, *sources: right_products(left, sources),
            left, terms[-1], *sources,
        )
    asked = asked_times(pairs, tm_size, pair_dev)
    first = first_time(asked, times_dev)
    slots = ready + [sum_of(terms[-1])]
    out = [pick(slots, slot_of(time, first, times_dev)) for time in asked]
    arrived = [
        shifted(jnp.stack(out[(d - 1) * pair_dev : d * pair_dev]), "tm", tm_size, d)
        for d in range(1, tm_size)
    ]
    sources = gather(choose_source(pairs, slots, arrived, tm_size, times_dev, pair_dev))
    return right_products(left, sources)


def late_source(pairs, source, final, times_dev):
    mine = pairs[lax.axis_index("tm"), 1] // times_dev == lax.axis_index("tm")
    return jnp.where(mine, sum_of(final)[None], source)


def solution(mesh):
    return jax.shard_map(
        local,
        mesh=mesh,
        in_specs=(
            P(("ens", "tm"), None, None, None, "space"),
            P("mom", None),
            P(),
            P(),
            P(("ens", "tm"), None, None, None, "space", None),
        ),
        out_specs=P(("ens", "tm"), "mom", None, "space", None),
        check_vma=False,
    )
```

time: 120 us -> 55.5 us (0.46)
  blocking collectives: 93.1 us -> 0 us
  waiting for transfers between devices: 0.01 us -> 18.3 us
  starting transfers between devices: 3.89 us -> 19.4 us
  matrix products: 15.5 us -> 0 us
  Pallas kernels: 0 us -> 10.2 us
  between operations: 0.38 us -> 2.8 us
  local copies, waits for them, and re-layouts: 5.32 us -> 3.34 us
    psum x1 -> x0, blocking collectives: 79.3 us -> none  [local(): whole = lax.psum(partial_value, 'space').astype(jnp.bfloat16)]
    ppermute x0 -> x12, starting transfers between devices: none -> 19.4 us  [the longest x10 17.8 us: swapped(): return lax.ppermute(value, 'space', [(i, i ^ by) for i in range(places)])]
    ppermute x0 -> x12, waiting for transfers between devices: none -> 18.3 us  [the longest x10 18.1 us: swapped(): return lax.ppermute(value, 'space', [(i, i ^ by) for i in range(places)])]
    dot_general x27 -> x0, matrix products: 15.5 us -> none  [the longest x4 3.57 us: elemental_terms(): lax.dot_general(imag_vec, imag_turned, contract_dims, preferred_element_t...]
    all_gather x1 -> x0, blocking collectives: 13.8 us -> none  [local(): lax.all_gather(mixed_peramb, 'space', axis=2, tiled=True)]
    pallas_call x0 -> x5, Pallas kernels: none -> 10.2 us  [the longest x2 8.4 us: partial_elementals(): pl.pallas_call(lambda *refs: elemental_kernel(slot, tm_size, places, dire...]
    all_to_all x1 -> x0, starting transfers between devices: 3.89 us -> none  [local(): lax.all_to_all(outgoing, 'tm', split_axis=0, concat_axis=0, tiled=True)]
    convert_element_type x2 -> x0, local copies, waits for them, and re-layouts: 3.68 us -> none  [the longest x1 2.54 us: local(): whole = lax.psum(partial_value, 'space').astype(jnp.bfloat16)]
  transfers between devices with their start and end apart: 1 -> 12, of which waited for: 0 -> 3; matrix products, arithmetic and copies ran while one was open for 3% -> 5% of each run, Pallas kernels for 0% -> 9%
where the time goes in v2:
time: 55.5 us; the launch traced here: 55.2 us
  starting transfers between devices  19.4 us (35%)
  waiting for transfers between devices  18.3 us (33%)
  Pallas kernels  10.2 us (18%)
  local copies, waits for them, and re-layouts  3.34 us (6%)
  between operations  2.8 us (5%)
  other arithmetic  1.19 us (2%)
    ppermute x10, waiting for transfers between devices, swapped(): return lax.ppermute(value, 'space', [(i, i ^ by) for i in range(places)])  18.1 us
    ppermute x10, starting transfers between devices, swapped(): return lax.ppermute(value, 'space', [(i, i ^ by) for i in range(places)])  17.8 us
    pallas_call x2, Pallas kernels, partial_elementals(): pl.pallas_call(lambda *refs: elemental_kernel(slot, tm_size, places, dire...  8.4 us
    unnamed x16, local copies, waits for them, and re-layouts  1.89 us
    ppermute x2, starting transfers between devices, shifted(): lax.ppermute(value, axis, [(i, (i + by) % size) for i in range(size)])  1.62 us
    slice x2, local copies, waits for them, and re-layouts, local(): late = (owners[0] == owners[1]) & (pairs[0, 1] != pairs[1, 1])  1.23 us
  transfers between devices with their start and end apart: 12, of which 3 were waited for; matrix products, arithmetic and copies ran while one was open for 5% of the time, Pallas kernels for 9%

profile of v2, /device:TPU:0, one launch (start us, length us, event | category | flops | bytes accessed | tf_op | source)
XLA Modules:
  0.0 55.2 jit_solution(14829405551980889339)
XLA Ops:
  0.0 5.1 %elementals.1 = (f32[2,2,64,256]{3,2,1,0:T(8,128)}, bf16[2,2,64,256]{3,2,1,0:T(8,128)(2,1)}, bf16[2,2,64,256]{3,2,1,0:T(8,128)(2,1)}, bf16[2,2,64,256]{3,2,1,0:T(8,128)(2,1)}) custom-call(s32[2,3]{1,0:T(2,128)} %refs_0_.5, s32[2,2]{1,0:T(2,128)} %refs_0_.7, bf16[2,2,3,256,512]{4,3,2,1,0:T(8,128)(2,1)} %refs_3_.1), custom_call_target="tpu_custom_call" | custom-call | tf_op jit(solution)/shard_map/elementals/pallas_call | solution.py:153
  5.1 3.1 %collective-permute-start.6 = (bf16[2,2,64,256]{3,2,1,0:T(8,128)(2,1)}, bf16[2,2,64,256]{3,2,1,0:T(8,128)(2,1)S(1)}, u32[]{:S(2)}, u32[]{:S(2)}) collective-permute-start(bf16[2,2,64,256]{3,2,1,0:T(8,128)(2,1)} %get-tuple-element.63), channel_id=1, source_target_pairs={{0,4},{4,0},{8,12},{12,8},{1,5},{5,1},{9,13},{13,9},{2,6},{6,2},{1... | collective-permute-start | bytes 393224 | tf_op jit(solution)/shard_map/ppermute | solution.py:278
  8.2 2.6 %collective-permute-start.7 = (bf16[2,2,64,256]{3,2,1,0:T(8,128)(2,1)}, bf16[2,2,64,256]{3,2,1,0:T(8,128)(2,1)S(1)}, u32[]{:S(2)}, u32[]{:S(2)}) collective-permute-start(bf16[2,2,64,256]{3,2,1,0:T(8,128)(2,1)} %get-tuple-element.64), channel_id=1, source_target_pairs={{0,8},{4,12},{8,0},{12,4},{1,9},{5,13},{9,1},{13,5},{2,10},{6,14},... | collective-permute-start | bytes 393224 | tf_op jit(solution)/shard_map/ppermute | solution.py:278
  10.8 0.0 collective-permute-start.8
  10.9 0.0 copy-start.1
  10.9 1.2 %copy-done.1 = bf16[1,2,4,4,64,256]{5,4,3,2,1,0:T(8,128)(2,1)S(1)} copy-done((bf16[1,2,4,4,64,256]{5,4,3,2,1,0:T(8,128)(2,1)S(1)}, bf16[1,2,4,4,64,256]{5,4,3,2,1,0:T(8,128)(2,1)}, u32[]{:S(2)}) %copy-start.1) | copy-done | bytes 1048600
  12.1 3.3 %elementals_mixing.1 = (bf16[1,2,32,256]{3,2,1,0:T(8,128)(2,1)S(1)}, f32[2,2,2,64,256]{4,3,2,1,0:T(8,128)S(1)}, bf16[2,2,2,64,256]{4,3,2,1,0:T(8,128)(2,1)S(1)}) custom-call(s32[2,3]{1,0:T(2,128)S(1)} %copy-done.3, s32[2,2]{1,0:T(2,128)S(1)} %copy-done.7, f32[4,4]{1,0:T(4,128)S(1)} %copy-done.4, bf16[2,2,3,256,512]{4,3,2,1,0:T(8,128)(2,1)S(1)} %copy-done, ...), custom_call_target="tpu_custom_call" | custom-call | tf_op jit(solution)/shard_map/elementals_mixing/pallas_call | solution.py:153
  15.4 0.9 %collective-permute-start.9 = (bf16[2,2,2,64,256]{4,3,2,1,0:T(8,128)(2,1)S(1)}, bf16[2,2,2,64,256]{4,3,2,1,0:T(8,128)(2,1)S(1)}, u32[]{:S(2)}, u32[]{:S(2)}) collective-permute-start(bf16[2,2,2,64,256]{4,3,2,1,0:T(8,128)(2,1)S(1)} %get-tuple-element.67), channel_id=1, source_target_pairs={{0,4},{4,0},{8,12},{12,8},{1,5},{5,1},{9,13},{13,9},{2,6},{6,2},{1... | collective-permute-start | bytes 786440 | tf_op jit(solution)/shard_map/ppermute | solution.py:278
  16.4 3.5 %collective-permute-start.3 = (bf16[1,1,2,32,256]{4,3,2,1,0:T(8,128)(2,1)S(1)}, bf16[1,1,2,32,256]{4,3,2,1,0:T(8,128)(2,1)S(1)}, u32[]{:S(2)}, u32[]{:S(2)}) collective-permute-start(bf16[1,1,2,32,256]{4,3,2,1,0:T(8,128)(2,1)S(1)} %bitcast.13), channel_id=1, source_target_pairs={{0,8},{4,12},{8,0},{12,4},{1,9},{5,13},{9,1},{13,5},{2,10},{6,14},... | collective-permute-start | bytes 98312 | tf_op jit(solution)/shard_map/ppermute | solution.py:278
  19.8 0.2 slice_reduce_fusion
  20.0 0.6 %fusion.2 = (s32[1,1]{1,0:T(1,128)}, s32[1,1]{1,0:T(1,128)}) fusion(s32[2,2]{1,0:T(2,128)S(1)} %copy-done.7), kind=kLoop, calls=%fused_computation.15 | loop fusion | bytes 16 | tf_op jit(solution)/shard_map/slice | solution.py:307
  20.7 2.9 %collective-permute-done.3 = bf16[1,1,2,32,256]{4,3,2,1,0:T(8,128)(2,1)S(1)} collective-permute-done((bf16[1,1,2,32,256]{4,3,2,1,0:T(8,128)(2,1)S(1)}, bf16[1,1,2,32,256]{4,3,2,1,0:T(8,128)(2,1)S(1)}, u32[]{:S(2)}, u32[]{:S(2)}) %collective-permute-start.3) | collective-permute-done | bytes 32800 | tf_op jit(solution)/shard_map/ppermute | solution.py:278
  23.6 3.1 %collective-permute-start.4 = (bf16[2,1,2,32,256]{4,3,2,1,0:T(8,128)(2,1)S(1)}, bf16[2,1,2,32,256]{4,3,2,1,0:T(8,128)(2,1)S(1)}, u32[]{:S(2)}, u32[]{:S(2)}) collective-permute-start(bf16[2,1,2,32,256]{4,3,2,1,0:T(8,128)(2,1)S(1)} %pad_maximum_fusion.1), channel_id=1, source_target_pairs={{0,4},{4,0},{8,12},{12,8},{1,5},{5,1},{9,13},{13,9},{2,6},{6,2},{1... | collective-permute-start | bytes 196616 | tf_op jit(solution)/shard_map/ppermute | solution.py:278
  26.8 0.0 collective-permute-done.6
  26.8 0.0 collective-permute-done.7
  26.8 0.1 add_convert_fusion.1.refs_3_.refs_1_
  26.9 1.6 %collective-permute-start.11 = (bf16[1,2,2,64,256]{4,3,2,1,0:T(8,128)(2,1)S(1)}, bf16[1,2,2,64,256]{4,3,2,1,0:T(8,128)(2,1)S(1)}, u32[]{:S(2)}, u32[]{:S(2)}) collective-permute-start(bf16[1,2,2,64,256]{4,3,2,1,0:T(8,128)(2,1)S(1)} %bitcast.12), channel_id=1, source_target_pairs={{0,2},{2,0},{1,3},{3,1},{4,6},{6,4},{5,7},{7,5},{8,10},{10,8},{9,1... | collective-permute-start | bytes 393224 | tf_op jit(solution)/shard_map/ppermute | solution.py:282
  28.4 0.6 %fusion.3 = (s32[1]{0:T(128)}, s32[1]{0:T(128)}) fusion(s32[2]{0:T(128)S(1)} %and_select_fusion), kind=kLoop, calls=%fused_computation.16 | loop fusion | bytes 16 | tf_op jit(solution)/shard_map/slice | solution.py:307
  31.6 0.1 collective-permute-start.5
  31.7 0.2 collective-permute-done.11.refs_2_
  31.9 0.6 %choose_source.1 = bf16[1,2,2,64,256]{4,3,2,1,0:T(8,128)(2,1)S(1)} custom-call(s32[2,2]{1,0:T(2,128)S(1)} %copy-done.7, bf16[2,2,64,256]{3,2,1,0:T(8,128)(2,1)S(1)} %add_convert_fusion.1.refs_3_.refs_1_, bf16[1,2,2,64,256]{4,3,2,1,0:T(8,128)(2,1)S(1)} %collective-permute-done.11.refs_2_), custom_call_target="tpu_custom_call" | custom-call | tf_op jit(solution)/shard_map/choose_source/pallas_call | solution.py:193
  32.5 0.1 collective-permute-start.12
  32.6 1.9 %collective-permute-start.13 = (bf16[1,2,2,64,256]{4,3,2,1,0:T(8,128)(2,1)S(1)}, bf16[1,2,2,64,256]{4,3,2,1,0:T(8,128)(2,1)S(1)}, u32[]{:S(2)}, u32[]{:S(2)}) collective-permute-start(bf16[1,2,2,64,256]{4,3,2,1,0:T(8,128)(2,1)S(1)} %choose_source.1), channel_id=1, source_target_pairs={{0,8},{4,12},{8,0},{12,4},{1,9},{5,13},{9,1},{13,5},{2,10},{6,14},... | collective-permute-start | bytes 393224 | tf_op jit(solution)/shard_map/ppermute | solution.py:278
  34.5 2.5 %collective-permute-start.14 = (bf16[1,2,2,64,256]{4,3,2,1,0:T(8,128)(2,1)S(1)}, bf16[1,2,2,64,256]{4,3,2,1,0:T(8,128)(2,1)S(1)}, u32[]{:S(2)}, u32[]{:S(2)}) collective-permute-start(bf16[1,2,2,64,256]{4,3,2,1,0:T(8,128)(2,1)S(1)} %choose_source.1), channel_id=1, source_target_pairs={{0,12},{4,8},{8,4},{12,0},{1,13},{5,9},{9,5},{13,1},{2,14},{6,10},... | collective-permute-start | bytes 393224 | tf_op jit(solution)/shard_map/ppermute | solution.py:278
  36.9 1.1 %convert_add_fusion = f32[2,2,2,64,256]{4,3,2,1,0:T(8,128)S(1)} fusion(f32[2,2,2,64,256]{4,3,2,1,0:T(8,128)} %copy-done.2, bf16[2,2,2,64,256]{4,3,2,1,0:T(8,128)(2,1)S(1)} %collective-permute-done.9), kind=kLoop, calls=%fused_computation.4 | loop fusion | flops 262144 | bytes 1310720 | tf_op jit(solution)/shard_map/add | solution.py:327
  38.1 0.1 collective-permute-start.10
  38.2 15.1 %collective-permute-done.10 = bf16[1,2,2,64,256]{4,3,2,1,0:T(8,128)(2,1)S(1)} collective-permute-done((bf16[1,2,2,64,256]{4,3,2,1,0:T(8,128)(2,1)S(1)}, bf16[1,2,2,64,256]{4,3,2,1,0:T(8,128)(2,1)S(1)}, u32[]{:S(2)}, u32[]{:S(2)}) %collective-permute-start.10) | collective-permute-done | bytes 131104 | tf_op jit(solution)/shard_map/ppermute | solution.py:278
  53.3 0.8 %left_products.1 = bf16[1,2,2,64,256]{4,3,2,1,0:T(8,128)(2,1)S(1)} custom-call(s32[2,2]{1,0:T(2,128)S(1)} %copy-done.7, bf16[4,1,2,32,256]{4,3,2,1,0:T(8,128)(2,1)S(1)} %pad_maximum_fusion.refs_1_, bf16[4,1,2,32,256]{4,3,2,1,0:T(8,128)(2,1)S(1)} %collective-permute-done.5.refs_2_, bf16[2,2,64,256]{3,2,1,0:T(8,128)(2,1)S(1)} %add_convert_fusion.1.refs_3_.refs_1_, ...), custom_call_target="tpu_custom_call" | custom-call | tf_op jit(solution)/shard_map/left_products/pallas_call | solution.py:235
  54.2 0.4 conditional.1
  54.2 0.3 right_products.2
  54.6 0.0 copy-start.6
  54.6 0.6 %copy-done.6 = bf16[1,2,2,64,256]{4,3,2,1,0:T(8,128)(2,1)} copy-done((bf16[1,2,2,64,256]{4,3,2,1,0:T(8,128)(2,1)}, bf16[1,2,2,64,256]{4,3,2,1,0:T(8,128)(2,1)S(1)}, u32[]{:S(2)}) %copy-start.6) | copy-done | bytes 131096
  (24 shorter events, 0.1 us)
Async XLA Ops:
  0.0 10.8 %copy-start = (bf16[2,2,3,256,512]{4,3,2,1,0:T(8,128)(2,1)S(1)}, bf16[2,2,3,256,512]{4,3,2,1,0:T(8,128)(2,1)}, u32[]{:S(2)}) copy-start(bf16[2,2,3,256,512]{4,3,2,1,0:T(8,128)(2,1)} %refs_3_.1) | copy-start | bytes 9437188
  0.0 10.8 %copy-start.3 = (s32[2,3]{1,0:T(2,128)S(1)}, s32[2,3]{1,0:T(2,128)}, u32[]{:S(2)}) copy-start(s32[2,3]{1,0:T(2,128)} %refs_0_.5) | copy-start | bytes 76
  0.0 10.8 %copy-start.7 = (s32[2,2]{1,0:T(2,128)S(1)}, s32[2,2]{1,0:T(2,128)}, u32[]{:S(2)}) copy-start(s32[2,2]{1,0:T(2,128)} %refs_0_.7) | copy-start | bytes 52
  0.0 10.8 %copy-start.4 = (f32[4,4]{1,0:T(4,128)S(1)}, f32[4,4]{1,0:T(4,128)}, u32[]{:S(2)}) copy-start(f32[4,4]{1,0:T(4,128)} %refs_2_.3) | copy-start | bytes 196
  5.1 21.6 %collective-permute-start.6 = (bf16[2,2,64,256]{3,2,1,0:T(8,128)(2,1)}, bf16[2,2,64,256]{3,2,1,0:T(8,128)(2,1)S(1)}, u32[]{:S(2)}, u32[]{:S(2)}) collective-permute-start(bf16[2,2,64,256]{3,2,1,0:T(8,128)(2,1)} %get-tuple-element.63), channel_id=1, source_target_pairs={{0,4},{4,0},{8,12},{12,8},{1,5},{5,1},{9,13},{13,9},{2,6},{6,2},{1... | collective-permute-start | bytes 393224 | tf_op jit(solution)/shard_map/ppermute | solution.py:278
  8.2 18.5 %collective-permute-start.7 = (bf16[2,2,64,256]{3,2,1,0:T(8,128)(2,1)}, bf16[2,2,64,256]{3,2,1,0:T(8,128)(2,1)S(1)}, u32[]{:S(2)}, u32[]{:S(2)}) collective-permute-start(bf16[2,2,64,256]{3,2,1,0:T(8,128)(2,1)} %get-tuple-element.64), channel_id=1, source_target_pairs={{0,8},{4,12},{8,0},{12,4},{1,9},{5,13},{9,1},{13,5},{2,10},{6,14},... | collective-permute-start | bytes 393224 | tf_op jit(solution)/shard_map/ppermute | solution.py:278
  10.8 15.9 %collective-permute-start.8 = (bf16[2,2,64,256]{3,2,1,0:T(8,128)(2,1)}, bf16[2,2,64,256]{3,2,1,0:T(8,128)(2,1)S(1)}, u32[]{:S(2)}, u32[]{:S(2)}) collective-permute-start(bf16[2,2,64,256]{3,2,1,0:T(8,128)(2,1)} %get-tuple-element.65), channel_id=1, source_target_pairs={{0,12},{4,8},{8,4},{12,0},{1,13},{5,9},{9,5},{13,1},{2,14},{6,10},... | collective-permute-start | bytes 393224 | tf_op jit(solution)/shard_map/ppermute | solution.py:278
  10.9 1.2 %copy-start.1 = (bf16[1,2,4,4,64,256]{5,4,3,2,1,0:T(8,128)(2,1)S(1)}, bf16[1,2,4,4,64,256]{5,4,3,2,1,0:T(8,128)(2,1)}, u32[]{:S(2)}) copy-start(bf16[1,2,4,4,64,256]{5,4,3,2,1,0:T(8,128)(2,1)} %refs_4_.1) | copy-start | bytes 3145732
  12.1 14.7 %copy-start.5 = (f32[2,2,64,256]{3,2,1,0:T(8,128)S(1)}, f32[2,2,64,256]{3,2,1,0:T(8,128)}, u32[]{:S(2)}) copy-start(f32[2,2,64,256]{3,2,1,0:T(8,128)} %get-tuple-element.62) | copy-start | bytes 786436
  15.4 11.5 %copy-start.2 = (f32[2,2,2,64,256]{4,3,2,1,0:T(8,128)}, f32[2,2,2,64,256]{4,3,2,1,0:T(8,128)S(1)}, u32[]{:S(2)}) copy-start(f32[2,2,2,64,256]{4,3,2,1,0:T(8,128)S(1)} %get-tuple-element.66) | copy-start | bytes 1572868
  15.4 21.5 %collective-permute-start.9 = (bf16[2,2,2,64,256]{4,3,2,1,0:T(8,128)(2,1)S(1)}, bf16[2,2,2,64,256]{4,3,2,1,0:T(8,128)(2,1)S(1)}, u32[]{:S(2)}, u32[]{:S(2)}) collective-permute-start(bf16[2,2,2,64,256]{4,3,2,1,0:T(8,128)(2,1)S(1)} %get-tuple-element.67), channel_id=1, source_target_pairs={{0,4},{4,0},{8,12},{12,8},{1,5},{5,1},{9,13},{13,9},{2,6},{6,2},{1... | collective-permute-start | bytes 786440 | tf_op jit(solution)/shard_map/ppermute | solution.py:278
  16.4 7.3 %collective-permute-start.3 = (bf16[1,1,2,32,256]{4,3,2,1,0:T(8,128)(2,1)S(1)}, bf16[1,1,2,32,256]{4,3,2,1,0:T(8,128)(2,1)S(1)}, u32[]{:S(2)}, u32[]{:S(2)}) collective-permute-start(bf16[1,1,2,32,256]{4,3,2,1,0:T(8,128)(2,1)S(1)} %bitcast.13), channel_id=1, source_target_pairs={{0,8},{4,12},{8,0},{12,4},{1,9},{5,13},{9,1},{13,5},{2,10},{6,14},... | collective-permute-start | bytes 98312 | tf_op jit(solution)/shard_map/ppermute | solution.py:278
  23.6 8.0 %collective-permute-start.4 = (bf16[2,1,2,32,256]{4,3,2,1,0:T(8,128)(2,1)S(1)}, bf16[2,1,2,32,256]{4,3,2,1,0:T(8,128)(2,1)S(1)}, u32[]{:S(2)}, u32[]{:S(2)}) collective-permute-start(bf16[2,1,2,32,256]{4,3,2,1,0:T(8,128)(2,1)S(1)} %pad_maximum_fusion.1), channel_id=1, source_target_pairs={{0,4},{4,0},{8,12},{12,8},{1,5},{5,1},{9,13},{13,9},{2,6},{6,2},{1... | collective-permute-start | bytes 196616 | tf_op jit(solution)/shard_map/ppermute | solution.py:278
  26.9 5.0 %collective-permute-start.11 = (bf16[1,2,2,64,256]{4,3,2,1,0:T(8,128)(2,1)S(1)}, bf16[1,2,2,64,256]{4,3,2,1,0:T(8,128)(2,1)S(1)}, u32[]{:S(2)}, u32[]{:S(2)}) collective-permute-start(bf16[1,2,2,64,256]{4,3,2,1,0:T(8,128)(2,1)S(1)} %bitcast.12), channel_id=1, source_target_pairs={{0,2},{2,0},{1,3},{3,1},{4,6},{6,4},{5,7},{7,5},{8,10},{10,8},{9,1... | collective-permute-start | bytes 393224 | tf_op jit(solution)/shard_map/ppermute | solution.py:282
  31.6 6.6 %collective-permute-start.5 = (bf16[4,1,2,32,256]{4,3,2,1,0:T(8,128)(2,1)S(1)}, bf16[4,1,2,32,256]{4,3,2,1,0:T(8,128)(2,1)S(1)}, u32[]{:S(2)}, u32[]{:S(2)}) collective-permute-start(bf16[4,1,2,32,256]{4,3,2,1,0:T(8,128)(2,1)S(1)} %pad_maximum_fusion.refs_1_), channel_id=1, source_target_pairs={{0,1},{1,0},{2,3},{3,2},{4,5},{5,4},{6,7},{7,6},{8,9},{9,8},{10,11... | collective-permute-start | bytes 393224 | tf_op jit(solution)/shard_map/ppermute | solution.py:282
  32.5 21.7 %collective-permute-start.12 = (bf16[1,2,2,64,256]{4,3,2,1,0:T(8,128)(2,1)S(1)}, bf16[1,2,2,64,256]{4,3,2,1,0:T(8,128)(2,1)S(1)}, u32[]{:S(2)}, u32[]{:S(2)}) collective-permute-start(bf16[1,2,2,64,256]{4,3,2,1,0:T(8,128)(2,1)S(1)} %choose_source.1), channel_id=1, source_target_pairs={{0,4},{4,0},{8,12},{12,8},{1,5},{5,1},{9,13},{13,9},{2,6},{6,2},{1... | collective-permute-start | bytes 393224 | tf_op jit(solution)/shard_map/ppermute | solution.py:278
  32.6 21.6 %collective-permute-start.13 = (bf16[1,2,2,64,256]{4,3,2,1,0:T(8,128)(2,1)S(1)}, bf16[1,2,2,64,256]{4,3,2,1,0:T(8,128)(2,1)S(1)}, u32[]{:S(2)}, u32[]{:S(2)}) collective-permute-start(bf16[1,2,2,64,256]{4,3,2,1,0:T(8,128)(2,1)S(1)} %choose_source.1), channel_id=1, source_target_pairs={{0,8},{4,12},{8,0},{12,4},{1,9},{5,13},{9,1},{13,5},{2,10},{6,14},... | collective-permute-start | bytes 393224 | tf_op jit(solution)/shard_map/ppermute | solution.py:278
  34.5 19.7 %collective-permute-start.14 = (bf16[1,2,2,64,256]{4,3,2,1,0:T(8,128)(2,1)S(1)}, bf16[1,2,2,64,256]{4,3,2,1,0:T(8,128)(2,1)S(1)}, u32[]{:S(2)}, u32[]{:S(2)}) collective-permute-start(bf16[1,2,2,64,256]{4,3,2,1,0:T(8,128)(2,1)S(1)} %choose_source.1), channel_id=1, source_target_pairs={{0,12},{4,8},{8,4},{12,0},{1,13},{5,9},{9,5},{13,1},{2,14},{6,10},... | collective-permute-start | bytes 393224 | tf_op jit(solution)/shard_map/ppermute | solution.py:278
  38.1 15.3 %collective-permute-start.10 = (bf16[1,2,2,64,256]{4,3,2,1,0:T(8,128)(2,1)S(1)}, bf16[1,2,2,64,256]{4,3,2,1,0:T(8,128)(2,1)S(1)}, u32[]{:S(2)}, u32[]{:S(2)}) collective-permute-start(bf16[1,2,2,64,256]{4,3,2,1,0:T(8,128)(2,1)S(1)} %slice.36), channel_id=1, source_target_pairs={{0,8},{4,12},{8,0},{12,4},{1,9},{5,13},{9,1},{13,5},{2,10},{6,14},... | collective-permute-start | bytes 393224 | tf_op jit(solution)/shard_map/ppermute | solution.py:278
  54.6 0.7 %copy-start.6 = (bf16[1,2,2,64,256]{4,3,2,1,0:T(8,128)(2,1)}, bf16[1,2,2,64,256]{4,3,2,1,0:T(8,128)(2,1)S(1)}, u32[]{:S(2)}) copy-start(bf16[1,2,2,64,256]{4,3,2,1,0:T(8,128)(2,1)S(1)} %get-tuple-element.99) | copy-start | bytes 393220

commit v3 on v2

--- a/solution.py
+++ b/solution.py
@@ -32,8 +32,10 @@
     ]
 
 
-def first_time(asked, times_dev):
+def first_time(pairs, tm_size, pair_dev, times_dev):
     group = lax.axis_index("tm")
+    asked = asked_times(pairs, tm_size, pair_dev)
+    asked += [pairs[group * pair_dev + p, 1] for p in range(pair_dev)]
     first = jnp.int32(0)
     for time in reversed(asked):
         first = jnp.where(lax.div(time, times_dev) == group, lax.rem(time, times_dev), first)
@@ -44,17 +46,28 @@
     return lax.rem(lax.rem(time, times_dev) - first + times_dev, times_dev)
 
 
+def whole_part(value, by):
+    return jnp.floor((value + 0.5) * (1.0 / by))
+
+
 def phases(momenta, moms, first_site, sites):
-    site = first_site + lax.broadcasted_iota(jnp.int32, (1, sites), 1)
-    xcoord = (site % LAT).astype(jnp.float32)
-    ycoord = (site // LAT % LAT).astype(jnp.float32)
-    zcoord = (site // (LAT * LAT)).astype(jnp.float32)
-    found = []
-    for m in range(moms):
-        px, py, pz = (momenta[m, k].astype(jnp.float32) for k in range(3))
-        angles = (px * xcoord + py * ycoord + pz * zcoord) * (2.0 * math.pi / LAT)
-        found.append((jnp.cos(angles), jnp.sin(angles)))
-    return found
+    shape = (2 * moms, sites)
+    row = lax.broadcasted_iota(jnp.int32, shape, 0)
+    site = (first_site + lax.broadcasted_iota(jnp.int32, shape, 1)).astype(jnp.float32)
+    zcoord = whole_part(site, LAT * LAT)
+    rest = site - zcoord * (LAT * LAT)
+    ycoord = whole_part(rest, LAT)
+    xcoord = rest - ycoord * LAT
+    turns = jnp.where(row % 2 == 0, 0.0, 0.75 * LAT)
+    for k, coord in enumerate((xcoord, ycoord, zcoord)):
+        component = momenta[moms - 1, k].astype(jnp.float32)
+        for m in reversed(range(moms - 1)):
+            component = jnp.where(row < 2 * (m + 1), momenta[m, k].astype(jnp.float32), component)
+        turns = turns + component * coord
+    turns = turns - LAT * whole_part(turns, LAT)
+    turns = jnp.where(turns < LAT / 2, turns, turns - LAT)
+    rows = jnp.cos(turns * (2.0 * math.pi / LAT))
+    return [(rows[2 * m : 2 * m + 1], rows[2 * m + 1 : 2 * m + 2]) for m in range(moms)]
 
 
 def mix(spin, per, out):
@@ -68,21 +81,33 @@
             out[q, c] = total.astype(out.dtype)
 
 
-def elemental_kernel(slot, tm_size, places, direct, parts, pair_dev, momenta, pairs, *refs):
+def elemental_kernel(slot, tm_size, places, direct, parts, pair_dev, momenta_hbm, pairs_hbm, *refs):
     mixing = parts > 0
     n_outs = places if direct else 2
     if mixing:
         spin, eig, per, mixed, *refs = refs
     else:
         eig, *refs = refs
-    outs, (held, acc, sems, *more) = refs[:n_outs], refs[n_outs:]
+    outs, (early, held, acc, momenta, pairs, sems, small, *more) = refs[:n_outs], refs[n_outs:]
     times, _, colours, vecs, sites = eig.shape
     moms, rows = outs[0].shape[-4], outs[0].shape[-2]
     place = lax.axis_index("space")
-    first = first_time(asked_times(pairs, tm_size, pair_dev), times)
+    pairs_copy = pltpu.make_async_copy(pairs_hbm, pairs, small.at[0])
+    momenta_copy = pltpu.make_async_copy(momenta_hbm, momenta, small.at[1])
+    pairs_copy.start()
+    momenta_copy.start()
+    ahead = [
+        pltpu.make_async_copy(eig.at[t, :, 0], early.at[t], sems.at[colours - 1 + t])
+        for t in range(times)
+    ]
+    for copy in ahead:
+        copy.start()
+    pairs_copy.wait()
+    first = first_time(pairs, tm_size, pair_dev, times)
     time = lax.rem(first + slot, times)
     copies = [
-        pltpu.make_async_copy(eig.at[time, :, c], held.at[c], sems.at[c]) for c in range(colours)
+        pltpu.make_async_copy(eig.at[time, :, c], held.at[c - 1], sems.at[c - 1])
+        for c in range(1, colours)
     ]
     for copy in copies:
         copy.start()
@@ -94,12 +119,18 @@
             per.at[:, :, :, :, pl.ds(start, take), :], per_held, per_sem
         )
         per_copy.start()
+    momenta_copy.wait()
     turns = phases(momenta, moms, place * sites, sites)
     for c in range(colours):
-        copies[c].wait()
-        both = held[c].reshape(2 * vecs, sites)
-        real_wide = held[c, 0].astype(jnp.float32)
-        imag_wide = held[c, 1].astype(jnp.float32)
+        if c == 0:
+            for copy in ahead:
+                copy.wait()
+        else:
+            copies[c - 1].wait()
+        pair = early.at[time] if c == 0 else held.at[c - 1]
+        both = pair[...].reshape(2 * vecs, sites)
+        real_wide = pair[0].astype(jnp.float32)
+        imag_wide = pair[1].astype(jnp.float32)
         for m, (cosine, sine) in enumerate(turns):
             real_turned = (cosine * real_wide + sine * imag_wide).astype(jnp.bfloat16)
             imag_turned = (cosine * imag_wide - sine * real_wide).astype(jnp.bfloat16)
@@ -125,7 +156,7 @@
 def partial_elementals(
     slot, momenta, pairs, eigvecs, tm_size, places, direct, pair_dev, mixing=None
 ):
-    _, _, colours, vecs, sites = eigvecs.shape
+    times, _, colours, vecs, sites = eigvecs.shape
     block = (momenta.shape[0], 2, vecs // places, vecs)
     if direct:
         shapes = [jax.ShapeDtypeStruct(block, jnp.float32)]
@@ -135,15 +166,19 @@
             jax.ShapeDtypeStruct((places // 2, *block), dtype) for dtype in (jnp.float32, jnp.bfloat16)
         ]
     scratch = [
-        pltpu.VMEM((colours, 2, vecs, sites), jnp.bfloat16),
+        pltpu.VMEM((times, 2, vecs, sites), jnp.bfloat16),
+        pltpu.VMEM((colours - 1, 2, vecs, sites), jnp.bfloat16),
         pltpu.VMEM((block[0], 2, vecs, vecs), jnp.float32),
-        pltpu.SemaphoreType.DMA((colours,)),
+        pltpu.SMEM(momenta.shape, jnp.int32),
+        pltpu.SMEM(pairs.shape, jnp.int32),
+        pltpu.SemaphoreType.DMA((colours - 1 + times,)),
+        pltpu.SemaphoreType.DMA((2,)),
     ]
-    ins, operands, parts = [SMEM, SMEM, HBM], (momenta, pairs, eigvecs), 0
+    ins, operands, parts = [HBM, HBM, HBM], (momenta, pairs, eigvecs), 0
     if mixing is not None:
         spin_weights, perambulators, parts = mixing
         count, _, sinks, sources, rows, _ = perambulators.shape
-        ins = [SMEM, SMEM, SMEM, HBM, HBM]
+        ins = [HBM, HBM, SMEM, HBM, HBM]
         operands = (momenta, pairs, spin_weights, eigvecs, perambulators)
         shapes.insert(0, jax.ShapeDtypeStruct((count, 2, rows // parts, vecs), jnp.bfloat16))
         scratch.append(
@@ -171,7 +206,7 @@
 def source_kernel(tm_size, times, pair_dev, n_slots, pairs, *refs):
     slots, arrived, out_ref = refs[:n_slots], refs[n_slots:-1], refs[-1]
     group = lax.axis_index("tm")
-    first = first_time(asked_times(pairs, tm_size, pair_dev), times)
+    first = first_time(pairs, tm_size, pair_dev, times)
     for p in range(pair_dev):
         source = pairs[group * pair_dev + p, 1]
         owner, slot = lax.div(source, times), slot_of(source, first, times)
@@ -211,7 +246,7 @@
         for n, d in enumerate(order):
             start = pl.multiple_of((lax.axis_index("space") ^ d) * rows + half * take, take)
             mixed[:, :, pl.ds(start, take), :] = pieces[n]
-    first = first_time(asked_times(pairs, tm_size, pair_dev), times)
+    first = first_time(pairs, tm_size, pair_dev, times)
     for q in range(pair_dev):
         slot = slot_of(pairs[lax.axis_index("tm") * pair_dev + q, 0], first, times)
         sink_ref[...] = added(terms)
@@ -305,15 +340,16 @@
     few = (tm_size - 1) * pair_dev == 1 and times_dev == 2
     owners = pairs[:, 1] // times_dev
     late = (owners[0] == owners[1]) & (pairs[0, 1] != pairs[1, 1])
-    terms, late_pairs = [], pairs
+    terms, inputs = [], (momenta, pairs, spin_weights, eigvecs, perambulators)
     for k in range(times_dev):
         last = k == times_dev - 1
         direct = k == 0 and places <= DIRECT
+        momenta, late_pairs, spin_weights, eigvecs, perambulators = inputs
         blocks = partial_elementals(
             k, momenta, late_pairs, eigvecs, tm_size, places, direct, pair_dev,
             (spin_weights, perambulators, parts) if last else None,
         )
-        late_pairs, blocks = lax.optimization_barrier((pairs, blocks))
+        inputs, blocks = lax.optimization_barrier((inputs, blocks))
         if last:
             mine, *blocks = blocks
         if direct:
@@ -352,7 +388,7 @@
             left, terms[-1], *sources,
         )
     asked = asked_times(pairs, tm_size, pair_dev)
-    first = first_time(asked, times_dev)
+    first = first_time(pairs, tm_size, pair_dev, times_dev)
     slots = ready + [sum_of(terms[-1])]
     out = [pick(slots, slot_of(time, first, times_dev)) for time in asked]
     arrived = [

time: 55.5 us -> 55.2 us (level)
  no operation moved by 1% of the time
where the time goes in v3:
time: 55.2 us; the launch traced here: 54.9 us
  starting transfers between devices  19.5 us (35%)
  waiting for transfers between devices  17.9 us (32%)
  Pallas kernels  10.2 us (18%)
  local copies, waits for them, and re-layouts  3.34 us (6%)
  between operations  2.8 us (5%)
  other arithmetic  1.19 us (2%)
    ppermute x10, starting transfers between devices, swapped(): return lax.ppermute(value, 'space', [(i, i ^ by) for i in range(places)])  17.8 us
    ppermute x10, waiting for transfers between devices, swapped(): return lax.ppermute(value, 'space', [(i, i ^ by) for i in range(places)])  17.7 us
    pallas_call x2, Pallas kernels, partial_elementals(): pl.pallas_call(lambda *refs: elemental_kernel(slot, tm_size, places, dire...  8.47 us
    unnamed x16, local copies, waits for them, and re-layouts  1.89 us
    ppermute x2, starting transfers between devices, shifted(): lax.ppermute(value, axis, [(i, (i + by) % size) for i in range(size)])  1.63 us
    slice x2, local copies, waits for them, and re-layouts, local(): late = (owners[0] == owners[1]) & (pairs[0, 1] != pairs[1, 1])  1.23 us
  transfers between devices with their start and end apart: 12, of which 3 were waited for; matrix products, arithmetic and copies ran while one was open for 5% of the time, Pallas kernels for 9%

profile of v3, /device:TPU:0, one launch (start us, length us, event | category | flops | bytes accessed | tf_op | source)
XLA Modules:
  0.0 54.9 jit_solution(6863695494565004089)
XLA Ops:
  0.0 4.8 %elementals.1 = (f32[2,2,64,256]{3,2,1,0:T(8,128)}, bf16[2,2,64,256]{3,2,1,0:T(8,128)(2,1)}, bf16[2,2,64,256]{3,2,1,0:T(8,128)(2,1)}, bf16[2,2,64,256]{3,2,1,0:T(8,128)(2,1)}) custom-call(s32[2,3]{1,0:T(2,128)} %refs_0_.4, s32[2,2]{1,0:T(2,128)} %refs_0_.6, bf16[2,2,3,256,512]{4,3,2,1,0:T(8,128)(2,1)} %refs_3_), custom_call_target="tpu_custom_call" | custom-call | tf_op jit(solution)/shard_map/elementals/pallas_call | solution.py:188
  4.8 3.2 %collective-permute-start.6 = (bf16[2,2,64,256]{3,2,1,0:T(8,128)(2,1)}, bf16[2,2,64,256]{3,2,1,0:T(8,128)(2,1)S(1)}, u32[]{:S(2)}, u32[]{:S(2)}) collective-permute-start(bf16[2,2,64,256]{3,2,1,0:T(8,128)(2,1)} %get-tuple-element.71), channel_id=1, source_target_pairs={{0,4},{4,0},{8,12},{12,8},{1,5},{5,1},{9,13},{13,9},{2,6},{6,2},{1... | collective-permute-start | bytes 393224 | tf_op jit(solution)/shard_map/ppermute | solution.py:313
  7.9 2.6 %collective-permute-start.7 = (bf16[2,2,64,256]{3,2,1,0:T(8,128)(2,1)}, bf16[2,2,64,256]{3,2,1,0:T(8,128)(2,1)S(1)}, u32[]{:S(2)}, u32[]{:S(2)}) collective-permute-start(bf16[2,2,64,256]{3,2,1,0:T(8,128)(2,1)} %get-tuple-element.72), channel_id=1, source_target_pairs={{0,8},{4,12},{8,0},{12,4},{1,9},{5,13},{9,1},{13,5},{2,10},{6,14},... | collective-permute-start | bytes 393224 | tf_op jit(solution)/shard_map/ppermute | solution.py:313
  10.5 0.0 collective-permute-start.8
  10.6 0.0 copy-start.1
  10.6 1.2 %copy-done.1 = bf16[1,2,4,4,64,256]{5,4,3,2,1,0:T(8,128)(2,1)S(1)} copy-done((bf16[1,2,4,4,64,256]{5,4,3,2,1,0:T(8,128)(2,1)S(1)}, bf16[1,2,4,4,64,256]{5,4,3,2,1,0:T(8,128)(2,1)}, u32[]{:S(2)}) %copy-start.1) | copy-done | bytes 1048600
  11.8 3.7 %elementals_mixing.1 = (bf16[1,2,32,256]{3,2,1,0:T(8,128)(2,1)S(1)}, f32[2,2,2,64,256]{4,3,2,1,0:T(8,128)S(1)}, bf16[2,2,2,64,256]{4,3,2,1,0:T(8,128)(2,1)S(1)}) custom-call(s32[2,3]{1,0:T(2,128)S(1)} %copy-done.3, s32[2,2]{1,0:T(2,128)S(1)} %copy-done.7, f32[4,4]{1,0:T(4,128)S(1)} %copy-done.4, bf16[2,2,3,256,512]{4,3,2,1,0:T(8,128)(2,1)S(1)} %copy-done, ...), custom_call_target="tpu_custom_call" | custom-call | tf_op jit(solution)/shard_map/elementals_mixing/pallas_call | solution.py:188
  15.5 0.9 %collective-permute-start.9 = (bf16[2,2,2,64,256]{4,3,2,1,0:T(8,128)(2,1)S(1)}, bf16[2,2,2,64,256]{4,3,2,1,0:T(8,128)(2,1)S(1)}, u32[]{:S(2)}, u32[]{:S(2)}) collective-permute-start(bf16[2,2,2,64,256]{4,3,2,1,0:T(8,128)(2,1)S(1)} %get-tuple-element.75), channel_id=1, source_target_pairs={{0,4},{4,0},{8,12},{12,8},{1,5},{5,1},{9,13},{13,9},{2,6},{6,2},{1... | collective-permute-start | bytes 786440 | tf_op jit(solution)/shard_map/ppermute | solution.py:313
  16.5 3.5 %collective-permute-start.3 = (bf16[1,1,2,32,256]{4,3,2,1,0:T(8,128)(2,1)S(1)}, bf16[1,1,2,32,256]{4,3,2,1,0:T(8,128)(2,1)S(1)}, u32[]{:S(2)}, u32[]{:S(2)}) collective-permute-start(bf16[1,1,2,32,256]{4,3,2,1,0:T(8,128)(2,1)S(1)} %bitcast.13), channel_id=1, source_target_pairs={{0,8},{4,12},{8,0},{12,4},{1,9},{5,13},{9,1},{13,5},{2,10},{6,14},... | collective-permute-start | bytes 98312 | tf_op jit(solution)/shard_map/ppermute | solution.py:313
  20.0 0.2 slice_reduce_fusion
  20.2 0.6 %fusion.2 = (s32[1,1]{1,0:T(1,128)}, s32[1,1]{1,0:T(1,128)}) fusion(s32[2,2]{1,0:T(2,128)S(1)} %copy-done.7), kind=kLoop, calls=%fused_computation.15 | loop fusion | bytes 16 | tf_op jit(solution)/shard_map/slice | solution.py:342
  20.8 2.5 %collective-permute-done.3 = bf16[1,1,2,32,256]{4,3,2,1,0:T(8,128)(2,1)S(1)} collective-permute-done((bf16[1,1,2,32,256]{4,3,2,1,0:T(8,128)(2,1)S(1)}, bf16[1,1,2,32,256]{4,3,2,1,0:T(8,128)(2,1)S(1)}, u32[]{:S(2)}, u32[]{:S(2)}) %collective-permute-start.3) | collective-permute-done | bytes 32800 | tf_op jit(solution)/shard_map/ppermute | solution.py:313
  23.3 3.1 %collective-permute-start.4 = (bf16[2,1,2,32,256]{4,3,2,1,0:T(8,128)(2,1)S(1)}, bf16[2,1,2,32,256]{4,3,2,1,0:T(8,128)(2,1)S(1)}, u32[]{:S(2)}, u32[]{:S(2)}) collective-permute-start(bf16[2,1,2,32,256]{4,3,2,1,0:T(8,128)(2,1)S(1)} %pad_maximum_fusion.1), channel_id=1, source_target_pairs={{0,4},{4,0},{8,12},{12,8},{1,5},{5,1},{9,13},{13,9},{2,6},{6,2},{1... | collective-permute-start | bytes 196616 | tf_op jit(solution)/shard_map/ppermute | solution.py:313
  26.5 0.0 collective-permute-done.6
  26.5 0.0 collective-permute-done.7
  26.5 0.1 add_convert_fusion.1.refs_3_.refs_1_
  26.6 1.6 %collective-permute-start.11 = (bf16[1,2,2,64,256]{4,3,2,1,0:T(8,128)(2,1)S(1)}, bf16[1,2,2,64,256]{4,3,2,1,0:T(8,128)(2,1)S(1)}, u32[]{:S(2)}, u32[]{:S(2)}) collective-permute-start(bf16[1,2,2,64,256]{4,3,2,1,0:T(8,128)(2,1)S(1)} %bitcast.12), channel_id=1, source_target_pairs={{0,2},{2,0},{1,3},{3,1},{4,6},{6,4},{5,7},{7,5},{8,10},{10,8},{9,1... | collective-permute-start | bytes 393224 | tf_op jit(solution)/shard_map/ppermute | solution.py:317
  28.1 0.6 %fusion.3 = (s32[1]{0:T(128)}, s32[1]{0:T(128)}) fusion(s32[2]{0:T(128)S(1)} %and_select_fusion), kind=kLoop, calls=%fused_computation.16 | loop fusion | bytes 16 | tf_op jit(solution)/shard_map/slice | solution.py:342
  31.3 0.1 collective-permute-start.5
  31.4 0.2 collective-permute-done.11.refs_2_
  31.6 0.6 %choose_source.1 = bf16[1,2,2,64,256]{4,3,2,1,0:T(8,128)(2,1)S(1)} custom-call(s32[2,2]{1,0:T(2,128)S(1)} %copy-done.7, bf16[2,2,64,256]{3,2,1,0:T(8,128)(2,1)S(1)} %add_convert_fusion.1.refs_3_.refs_1_, bf16[1,2,2,64,256]{4,3,2,1,0:T(8,128)(2,1)S(1)} %collective-permute-done.11.refs_2_), custom_call_target="tpu_custom_call" | custom-call | tf_op jit(solution)/shard_map/choose_source/pallas_call | solution.py:228
  32.2 0.1 collective-permute-start.12
  32.3 1.9 %collective-permute-start.13 = (bf16[1,2,2,64,256]{4,3,2,1,0:T(8,128)(2,1)S(1)}, bf16[1,2,2,64,256]{4,3,2,1,0:T(8,128)(2,1)S(1)}, u32[]{:S(2)}, u32[]{:S(2)}) collective-permute-start(bf16[1,2,2,64,256]{4,3,2,1,0:T(8,128)(2,1)S(1)} %choose_source.1), channel_id=1, source_target_pairs={{0,8},{4,12},{8,0},{12,4},{1,9},{5,13},{9,1},{13,5},{2,10},{6,14},... | collective-permute-start | bytes 393224 | tf_op jit(solution)/shard_map/ppermute | solution.py:313
  34.2 2.5 %collective-permute-start.14 = (bf16[1,2,2,64,256]{4,3,2,1,0:T(8,128)(2,1)S(1)}, bf16[1,2,2,64,256]{4,3,2,1,0:T(8,128)(2,1)S(1)}, u32[]{:S(2)}, u32[]{:S(2)}) collective-permute-start(bf16[1,2,2,64,256]{4,3,2,1,0:T(8,128)(2,1)S(1)} %choose_source.1), channel_id=1, source_target_pairs={{0,12},{4,8},{8,4},{12,0},{1,13},{5,9},{9,5},{13,1},{2,14},{6,10},... | collective-permute-start | bytes 393224 | tf_op jit(solution)/shard_map/ppermute | solution.py:313
  36.6 1.1 %convert_add_fusion = f32[2,2,2,64,256]{4,3,2,1,0:T(8,128)S(1)} fusion(f32[2,2,2,64,256]{4,3,2,1,0:T(8,128)} %copy-done.2, bf16[2,2,2,64,256]{4,3,2,1,0:T(8,128)(2,1)S(1)} %collective-permute-done.9), kind=kLoop, calls=%fused_computation.4 | loop fusion | flops 262144 | bytes 1310720 | tf_op jit(solution)/shard_map/add | solution.py:363
  37.8 0.1 collective-permute-start.10
  37.9 15.1 %collective-permute-done.10 = bf16[1,2,2,64,256]{4,3,2,1,0:T(8,128)(2,1)S(1)} collective-permute-done((bf16[1,2,2,64,256]{4,3,2,1,0:T(8,128)(2,1)S(1)}, bf16[1,2,2,64,256]{4,3,2,1,0:T(8,128)(2,1)S(1)}, u32[]{:S(2)}, u32[]{:S(2)}) %collective-permute-start.10) | collective-permute-done | bytes 131104 | tf_op jit(solution)/shard_map/ppermute | solution.py:313
  53.0 0.8 %left_products.1 = bf16[1,2,2,64,256]{4,3,2,1,0:T(8,128)(2,1)S(1)} custom-call(s32[2,2]{1,0:T(2,128)S(1)} %copy-done.7, bf16[4,1,2,32,256]{4,3,2,1,0:T(8,128)(2,1)S(1)} %pad_maximum_fusion.refs_1_, bf16[4,1,2,32,256]{4,3,2,1,0:T(8,128)(2,1)S(1)} %collective-permute-done.5.refs_2_, bf16[2,2,64,256]{3,2,1,0:T(8,128)(2,1)S(1)} %add_convert_fusion.1.refs_3_.refs_1_, ...), custom_call_target="tpu_custom_call" | custom-call | tf_op jit(solution)/shard_map/left_products/pallas_call | solution.py:270
  53.9 0.4 conditional.1
  53.9 0.4 right_products.2
  54.3 0.0 copy-start.6
  54.3 0.6 %copy-done.6 = bf16[1,2,2,64,256]{4,3,2,1,0:T(8,128)(2,1)} copy-done((bf16[1,2,2,64,256]{4,3,2,1,0:T(8,128)(2,1)}, bf16[1,2,2,64,256]{4,3,2,1,0:T(8,128)(2,1)S(1)}, u32[]{:S(2)}) %copy-start.6) | copy-done | bytes 131096
  (24 shorter events, 0.1 us)
Async XLA Ops:
  0.0 10.5 %copy-start = (bf16[2,2,3,256,512]{4,3,2,1,0:T(8,128)(2,1)S(1)}, bf16[2,2,3,256,512]{4,3,2,1,0:T(8,128)(2,1)}, u32[]{:S(2)}) copy-start(bf16[2,2,3,256,512]{4,3,2,1,0:T(8,128)(2,1)} %refs_3_) | copy-start | bytes 9437188
  0.0 10.5 %copy-start.3 = (s32[2,3]{1,0:T(2,128)S(1)}, s32[2,3]{1,0:T(2,128)}, u32[]{:S(2)}) copy-start(s32[2,3]{1,0:T(2,128)} %refs_0_.4) | copy-start | bytes 76
  0.0 10.5 %copy-start.7 = (s32[2,2]{1,0:T(2,128)S(1)}, s32[2,2]{1,0:T(2,128)}, u32[]{:S(2)}) copy-start(s32[2,2]{1,0:T(2,128)} %refs_0_.6) | copy-start | bytes 52
  0.0 10.6 %copy-start.4 = (f32[4,4]{1,0:T(4,128)S(1)}, f32[4,4]{1,0:T(4,128)}, u32[]{:S(2)}) copy-start(f32[4,4]{1,0:T(4,128)} %refs_2_.2) | copy-start | bytes 196
  4.8 21.7 %collective-permute-start.6 = (bf16[2,2,64,256]{3,2,1,0:T(8,128)(2,1)}, bf16[2,2,64,256]{3,2,1,0:T(8,128)(2,1)S(1)}, u32[]{:S(2)}, u32[]{:S(2)}) collective-permute-start(bf16[2,2,64,256]{3,2,1,0:T(8,128)(2,1)} %get-tuple-element.71), channel_id=1, source_target_pairs={{0,4},{4,0},{8,12},{12,8},{1,5},{5,1},{9,13},{13,9},{2,6},{6,2},{1... | collective-permute-start | bytes 393224 | tf_op jit(solution)/shard_map/ppermute | solution.py:313
  7.9 18.5 %collective-permute-start.7 = (bf16[2,2,64,256]{3,2,1,0:T(8,128)(2,1)}, bf16[2,2,64,256]{3,2,1,0:T(8,128)(2,1)S(1)}, u32[]{:S(2)}, u32[]{:S(2)}) collective-permute-start(bf16[2,2,64,256]{3,2,1,0:T(8,128)(2,1)} %get-tuple-element.72), channel_id=1, source_target_pairs={{0,8},{4,12},{8,0},{12,4},{1,9},{5,13},{9,1},{13,5},{2,10},{6,14},... | collective-permute-start | bytes 393224 | tf_op jit(solution)/shard_map/ppermute | solution.py:313
  10.5 15.9 %collective-permute-start.8 = (bf16[2,2,64,256]{3,2,1,0:T(8,128)(2,1)}, bf16[2,2,64,256]{3,2,1,0:T(8,128)(2,1)S(1)}, u32[]{:S(2)}, u32[]{:S(2)}) collective-permute-start(bf16[2,2,64,256]{3,2,1,0:T(8,128)(2,1)} %get-tuple-element.73), channel_id=1, source_target_pairs={{0,12},{4,8},{8,4},{12,0},{1,13},{5,9},{9,5},{13,1},{2,14},{6,10},... | collective-permute-start | bytes 393224 | tf_op jit(solution)/shard_map/ppermute | solution.py:313
  10.6 1.2 %copy-start.1 = (bf16[1,2,4,4,64,256]{5,4,3,2,1,0:T(8,128)(2,1)S(1)}, bf16[1,2,4,4,64,256]{5,4,3,2,1,0:T(8,128)(2,1)}, u32[]{:S(2)}) copy-start(bf16[1,2,4,4,64,256]{5,4,3,2,1,0:T(8,128)(2,1)} %refs_4_) | copy-start | bytes 3145732
  11.8 14.7 %copy-start.5 = (f32[2,2,64,256]{3,2,1,0:T(8,128)S(1)}, f32[2,2,64,256]{3,2,1,0:T(8,128)}, u32[]{:S(2)}) copy-start(f32[2,2,64,256]{3,2,1,0:T(8,128)} %get-tuple-element.70) | copy-start | bytes 786436
  15.5 11.0 %copy-start.2 = (f32[2,2,2,64,256]{4,3,2,1,0:T(8,128)}, f32[2,2,2,64,256]{4,3,2,1,0:T(8,128)S(1)}, u32[]{:S(2)}) copy-start(f32[2,2,2,64,256]{4,3,2,1,0:T(8,128)S(1)} %get-tuple-element.74) | copy-start | bytes 1572868
  15.5 21.1 %collective-permute-start.9 = (bf16[2,2,2,64,256]{4,3,2,1,0:T(8,128)(2,1)S(1)}, bf16[2,2,2,64,256]{4,3,2,1,0:T(8,128)(2,1)S(1)}, u32[]{:S(2)}, u32[]{:S(2)}) collective-permute-start(bf16[2,2,2,64,256]{4,3,2,1,0:T(8,128)(2,1)S(1)} %get-tuple-element.75), channel_id=1, source_target_pairs={{0,4},{4,0},{8,12},{12,8},{1,5},{5,1},{9,13},{13,9},{2,6},{6,2},{1... | collective-permute-start | bytes 786440 | tf_op jit(solution)/shard_map/ppermute | solution.py:313
  16.5 6.9 %collective-permute-start.3 = (bf16[1,1,2,32,256]{4,3,2,1,0:T(8,128)(2,1)S(1)}, bf16[1,1,2,32,256]{4,3,2,1,0:T(8,128)(2,1)S(1)}, u32[]{:S(2)}, u32[]{:S(2)}) collective-permute-start(bf16[1,1,2,32,256]{4,3,2,1,0:T(8,128)(2,1)S(1)} %bitcast.13), channel_id=1, source_target_pairs={{0,8},{4,12},{8,0},{12,4},{1,9},{5,13},{9,1},{13,5},{2,10},{6,14},... | collective-permute-start | bytes 98312 | tf_op jit(solution)/shard_map/ppermute | solution.py:313
  23.3 8.0 %collective-permute-start.4 = (bf16[2,1,2,32,256]{4,3,2,1,0:T(8,128)(2,1)S(1)}, bf16[2,1,2,32,256]{4,3,2,1,0:T(8,128)(2,1)S(1)}, u32[]{:S(2)}, u32[]{:S(2)}) collective-permute-start(bf16[2,1,2,32,256]{4,3,2,1,0:T(8,128)(2,1)S(1)} %pad_maximum_fusion.1), channel_id=1, source_target_pairs={{0,4},{4,0},{8,12},{12,8},{1,5},{5,1},{9,13},{13,9},{2,6},{6,2},{1... | collective-permute-start | bytes 196616 | tf_op jit(solution)/shard_map/ppermute | solution.py:313
  26.6 5.0 %collective-permute-start.11 = (bf16[1,2,2,64,256]{4,3,2,1,0:T(8,128)(2,1)S(1)}, bf16[1,2,2,64,256]{4,3,2,1,0:T(8,128)(2,1)S(1)}, u32[]{:S(2)}, u32[]{:S(2)}) collective-permute-start(bf16[1,2,2,64,256]{4,3,2,1,0:T(8,128)(2,1)S(1)} %bitcast.12), channel_id=1, source_target_pairs={{0,2},{2,0},{1,3},{3,1},{4,6},{6,4},{5,7},{7,5},{8,10},{10,8},{9,1... | collective-permute-start | bytes 393224 | tf_op jit(solution)/shard_map/ppermute | solution.py:317
  31.3 6.5 %collective-permute-start.5 = (bf16[4,1,2,32,256]{4,3,2,1,0:T(8,128)(2,1)S(1)}, bf16[4,1,2,32,256]{4,3,2,1,0:T(8,128)(2,1)S(1)}, u32[]{:S(2)}, u32[]{:S(2)}) collective-permute-start(bf16[4,1,2,32,256]{4,3,2,1,0:T(8,128)(2,1)S(1)} %pad_maximum_fusion.refs_1_), channel_id=1, source_target_pairs={{0,1},{1,0},{2,3},{3,2},{4,5},{5,4},{6,7},{7,6},{8,9},{9,8},{10,11... | collective-permute-start | bytes 393224 | tf_op jit(solution)/shard_map/ppermute | solution.py:317
  32.2 21.7 %collective-permute-start.12 = (bf16[1,2,2,64,256]{4,3,2,1,0:T(8,128)(2,1)S(1)}, bf16[1,2,2,64,256]{4,3,2,1,0:T(8,128)(2,1)S(1)}, u32[]{:S(2)}, u32[]{:S(2)}) collective-permute-start(bf16[1,2,2,64,256]{4,3,2,1,0:T(8,128)(2,1)S(1)} %choose_source.1), channel_id=1, source_target_pairs={{0,4},{4,0},{8,12},{12,8},{1,5},{5,1},{9,13},{13,9},{2,6},{6,2},{1... | collective-permute-start | bytes 393224 | tf_op jit(solution)/shard_map/ppermute | solution.py:313
  32.3 21.6 %collective-permute-start.13 = (bf16[1,2,2,64,256]{4,3,2,1,0:T(8,128)(2,1)S(1)}, bf16[1,2,2,64,256]{4,3,2,1,0:T(8,128)(2,1)S(1)}, u32[]{:S(2)}, u32[]{:S(2)}) collective-permute-start(bf16[1,2,2,64,256]{4,3,2,1,0:T(8,128)(2,1)S(1)} %choose_source.1), channel_id=1, source_target_pairs={{0,8},{4,12},{8,0},{12,4},{1,9},{5,13},{9,1},{13,5},{2,10},{6,14},... | collective-permute-start | bytes 393224 | tf_op jit(solution)/shard_map/ppermute | solution.py:313
  34.2 19.7 %collective-permute-start.14 = (bf16[1,2,2,64,256]{4,3,2,1,0:T(8,128)(2,1)S(1)}, bf16[1,2,2,64,256]{4,3,2,1,0:T(8,128)(2,1)S(1)}, u32[]{:S(2)}, u32[]{:S(2)}) collective-permute-start(bf16[1,2,2,64,256]{4,3,2,1,0:T(8,128)(2,1)S(1)} %choose_source.1), channel_id=1, source_target_pairs={{0,12},{4,8},{8,4},{12,0},{1,13},{5,9},{9,5},{13,1},{2,14},{6,10},... | collective-permute-start | bytes 393224 | tf_op jit(solution)/shard_map/ppermute | solution.py:313
  37.8 15.3 %collective-permute-start.10 = (bf16[1,2,2,64,256]{4,3,2,1,0:T(8,128)(2,1)S(1)}, bf16[1,2,2,64,256]{4,3,2,1,0:T(8,128)(2,1)S(1)}, u32[]{:S(2)}, u32[]{:S(2)}) collective-permute-start(bf16[1,2,2,64,256]{4,3,2,1,0:T(8,128)(2,1)S(1)} %slice.36), channel_id=1, source_target_pairs={{0,8},{4,12},{8,0},{12,4},{1,9},{5,13},{9,1},{13,5},{2,10},{6,14},... | collective-permute-start | bytes 393224 | tf_op jit(solution)/shard_map/ppermute | solution.py:313
  54.3 0.7 %copy-start.6 = (bf16[1,2,2,64,256]{4,3,2,1,0:T(8,128)(2,1)}, bf16[1,2,2,64,256]{4,3,2,1,0:T(8,128)(2,1)S(1)}, u32[]{:S(2)}) copy-start(bf16[1,2,2,64,256]{4,3,2,1,0:T(8,128)(2,1)S(1)} %get-tuple-element.107) | copy-start | bytes 393220

commit v4 on v3

--- a/solution.py
+++ b/solution.py
@@ -8,7 +8,7 @@
 from jax.sharding import PartitionSpec as P
 
 LAT = 48
-DIRECT = 4
+DIRECT = 0
 NT = (((1,), (1,)), ((), ()))
 NN = (((1,), (0,)), ((), ()))
 SMEM = pl.BlockSpec(memory_space=pltpu.SMEM)
@@ -191,7 +191,7 @@
         out_specs=[VMEM] * len(shapes),
         out_shape=shapes,
         scratch_shapes=scratch,
-        compiler_params=LARGE if parts else None,
+        compiler_params=LARGE if slot else None,
         name="elementals_mixing" if parts else "elementals",
     )(*operands)
 
@@ -342,15 +342,14 @@
     late = (owners[0] == owners[1]) & (pairs[0, 1] != pairs[1, 1])
     terms, inputs = [], (momenta, pairs, spin_weights, eigvecs, perambulators)
     for k in range(times_dev):
-        last = k == times_dev - 1
         direct = k == 0 and places <= DIRECT
         momenta, late_pairs, spin_weights, eigvecs, perambulators = inputs
         blocks = partial_elementals(
             k, momenta, late_pairs, eigvecs, tm_size, places, direct, pair_dev,
-            (spin_weights, perambulators, parts) if last else None,
+            (spin_weights, perambulators, parts) if k == times_dev - 1 else None,
         )
         inputs, blocks = lax.optimization_barrier((inputs, blocks))
-        if last:
+        if k == times_dev - 1:
             mine, *blocks = blocks
         if direct:
             own, *sends = blocks

time: 55.2 us -> 55.9 us (1.013)
  local copies, waits for them, and re-layouts: 3.34 us -> 4.16 us
    ppermute x10 -> x9, waiting for transfers between devices: 17.7 us -> 16.2 us  [swapped(): return lax.ppermute(value, 'space', [(i, i ^ by) for i in range(places)])]
    ppermute x2, waiting for transfers between devices: 0.2 us -> 1.22 us  [shifted(): lax.ppermute(value, axis, [(i, (i + by) % size) for i in range(size)])]
    unnamed x16 -> x18, local copies, waits for them, and re-layouts: 1.89 us -> 2.7 us
    ppermute x10 -> x9, starting transfers between devices: 17.8 us -> 18.2 us  [swapped(): return lax.ppermute(value, 'space', [(i, i ^ by) for i in range(places)])]
    add x1 -> x2, other arithmetic: 1.09 us -> 1.17 us  [local(): total = kept + received.astype(jnp.float32)]
  transfers between devices with their start and end apart: 12 -> 11, of which waited for: 3 -> 6; matrix products, arithmetic and copies ran while one was open for 5% -> 5% of each run, Pallas kernels for 9% -> 3%
where the time goes in v4:
time: 55.9 us; the launch traced here: 55.7 us
  starting transfers between devices  19.7 us (35%)
  waiting for transfers between devices  17.5 us (31%)
  Pallas kernels  10.3 us (18%)
  local copies, waits for them, and re-layouts  4.16 us (7%)
  between operations  2.77 us (5%)
  other arithmetic  1.23 us (2%)
    ppermute x9, starting transfers between devices, swapped(): return lax.ppermute(value, 'space', [(i, i ^ by) for i in range(places)])  18.2 us
    ppermute x9, waiting for transfers between devices, swapped(): return lax.ppermute(value, 'space', [(i, i ^ by) for i in range(places)])  16.2 us
    pallas_call x2, Pallas kernels, partial_elementals(): pl.pallas_call(lambda *refs: elemental_kernel(slot, tm_size, places, dire...  8.56 us
    unnamed x18, local copies, waits for them, and re-layouts  2.7 us
    ppermute x2, starting transfers between devices, shifted(): lax.ppermute(value, axis, [(i, (i + by) % size) for i in range(size)])  1.53 us
    slice x2, local copies, waits for them, and re-layouts, local(): late = (owners[0] == owners[1]) & (pairs[0, 1] != pairs[1, 1])  1.23 us
    ppermute x2, waiting for transfers between devices, shifted(): lax.ppermute(value, axis, [(i, (i + by) % size) for i in range(size)])  1.22 us
    add x2, other arithmetic, local(): total = kept + received.astype(jnp.float32)  1.17 us
  transfers between devices with their start and end apart: 11, of which 6 were waited for; matrix products, arithmetic and copies ran while one was open for 5% of the time, Pallas kernels for 3%

profile of v4, /device:TPU:0, one launch (start us, length us, event | category | flops | bytes accessed | tf_op | source)
XLA Modules:
  0.0 55.7 jit_solution(4768430146696102045)
XLA Ops:
  0.0 4.8 %elementals.1 = (f32[2,2,2,64,256]{4,3,2,1,0:T(8,128)}, bf16[2,2,2,64,256]{4,3,2,1,0:T(8,128)(2,1)}) custom-call(s32[2,3]{1,0:T(2,128)} %refs_0_.4, s32[2,2]{1,0:T(2,128)} %refs_0_.6, bf16[2,2,3,256,512]{4,3,2,1,0:T(8,128)(2,1)} %refs_3_), custom_call_target="tpu_custom_call" | custom-call | tf_op jit(solution)/shard_map/elementals/pallas_call | solution.py:188
  4.9 0.0 copy-start.1
  4.9 1.2 %copy-done.1 = bf16[1,2,4,4,64,256]{5,4,3,2,1,0:T(8,128)(2,1)S(1)} copy-done((bf16[1,2,4,4,64,256]{5,4,3,2,1,0:T(8,128)(2,1)S(1)}, bf16[1,2,4,4,64,256]{5,4,3,2,1,0:T(8,128)(2,1)}, u32[]{:S(2)}) %copy-start.1) | copy-done | bytes 1048600
  6.1 3.7 %elementals_mixing.1 = (bf16[1,2,32,256]{3,2,1,0:T(8,128)(2,1)S(1)}, f32[2,2,2,64,256]{4,3,2,1,0:T(8,128)S(1)}, bf16[2,2,2,64,256]{4,3,2,1,0:T(8,128)(2,1)S(1)}) custom-call(s32[2,3]{1,0:T(2,128)S(1)} %copy-done.3, s32[2,2]{1,0:T(2,128)S(1)} %copy-done.7, f32[4,4]{1,0:T(4,128)S(1)} %copy-done.4, bf16[2,2,3,256,512]{4,3,2,1,0:T(8,128)(2,1)S(1)} %copy-done, ...), custom_call_target="tpu_custom_call" | custom-call | tf_op jit(solution)/shard_map/elementals_mixing/pallas_call | solution.py:188
  9.9 0.8 %copy-done.2 = f32[2,2,2,64,256]{4,3,2,1,0:T(8,128)} copy-done((f32[2,2,2,64,256]{4,3,2,1,0:T(8,128)}, f32[2,2,2,64,256]{4,3,2,1,0:T(8,128)S(1)}, u32[]{:S(2)}) %copy-start.2) | copy-done | bytes 524312
  10.7 3.1 %collective-permute-start.8 = (bf16[2,2,2,64,256]{4,3,2,1,0:T(8,128)(2,1)S(1)}, bf16[2,2,2,64,256]{4,3,2,1,0:T(8,128)(2,1)S(1)}, u32[]{:S(2)}, u32[]{:S(2)}) collective-permute-start(bf16[2,2,2,64,256]{4,3,2,1,0:T(8,128)(2,1)S(1)} %get-tuple-element.67), channel_id=1, source_target_pairs={{0,4},{4,0},{8,12},{12,8},{1,5},{5,1},{9,13},{13,9},{2,6},{6,2},{1... | collective-permute-start | bytes 786440 | tf_op jit(solution)/shard_map/ppermute | solution.py:313
  13.8 2.6 %collective-permute-start.3 = (bf16[1,1,2,32,256]{4,3,2,1,0:T(8,128)(2,1)S(1)}, bf16[1,1,2,32,256]{4,3,2,1,0:T(8,128)(2,1)S(1)}, u32[]{:S(2)}, u32[]{:S(2)}) collective-permute-start(bf16[1,1,2,32,256]{4,3,2,1,0:T(8,128)(2,1)S(1)} %bitcast.14), channel_id=1, source_target_pairs={{0,8},{4,12},{8,0},{12,4},{1,9},{5,13},{9,1},{13,5},{2,10},{6,14},... | collective-permute-start | bytes 98312 | tf_op jit(solution)/shard_map/ppermute | solution.py:313
  16.4 0.4 collective-permute-start.6
  16.8 0.2 slice_reduce_fusion
  17.0 0.6 %fusion.3 = (s32[1,1]{1,0:T(1,128)}, s32[1,1]{1,0:T(1,128)}) fusion(s32[2,2]{1,0:T(2,128)S(1)} %copy-done.7), kind=kLoop, calls=%fused_computation.18 | loop fusion | bytes 16 | tf_op jit(solution)/shard_map/slice | solution.py:342
  17.6 3.5 %collective-permute-done.3 = bf16[1,1,2,32,256]{4,3,2,1,0:T(8,128)(2,1)S(1)} collective-permute-done((bf16[1,1,2,32,256]{4,3,2,1,0:T(8,128)(2,1)S(1)}, bf16[1,1,2,32,256]{4,3,2,1,0:T(8,128)(2,1)S(1)}, u32[]{:S(2)}, u32[]{:S(2)}) %collective-permute-start.3) | collective-permute-done | bytes 32800 | tf_op jit(solution)/shard_map/ppermute | solution.py:313
  21.2 3.6 %collective-permute-start.4 = (bf16[2,1,2,32,256]{4,3,2,1,0:T(8,128)(2,1)S(1)}, bf16[2,1,2,32,256]{4,3,2,1,0:T(8,128)(2,1)S(1)}, u32[]{:S(2)}, u32[]{:S(2)}) collective-permute-start(bf16[2,1,2,32,256]{4,3,2,1,0:T(8,128)(2,1)S(1)} %pad_maximum_fusion.1), channel_id=1, source_target_pairs={{0,4},{4,0},{8,12},{12,8},{1,5},{5,1},{9,13},{13,9},{2,6},{6,2},{1... | collective-permute-start | bytes 196616 | tf_op jit(solution)/shard_map/ppermute | solution.py:313
  24.7 2.4 %collective-permute-done.6 = bf16[2,2,2,64,256]{4,3,2,1,0:T(8,128)(2,1)S(1)} collective-permute-done((bf16[2,2,2,64,256]{4,3,2,1,0:T(8,128)(2,1)S(1)}, bf16[2,2,2,64,256]{4,3,2,1,0:T(8,128)(2,1)S(1)}, u32[]{:S(2)}, u32[]{:S(2)}) %collective-permute-start.6) | collective-permute-done | bytes 262176 | tf_op jit(solution)/shard_map/ppermute | solution.py:313
  27.1 0.1 convert_add_fusion.1
  27.2 2.8 %collective-permute-start.7 = (bf16[1,2,2,64,256]{4,3,2,1,0:T(8,128)(2,1)S(1)}, bf16[1,2,2,64,256]{4,3,2,1,0:T(8,128)(2,1)S(1)}, u32[]{:S(2)}, u32[]{:S(2)}) collective-permute-start(bf16[1,2,2,64,256]{4,3,2,1,0:T(8,128)(2,1)S(1)} %slice.54), channel_id=1, source_target_pairs={{0,8},{4,12},{8,0},{12,4},{1,9},{5,13},{9,1},{13,5},{2,10},{6,14},... | collective-permute-start | bytes 393224 | tf_op jit(solution)/shard_map/ppermute | solution.py:313
  30.0 0.6 %fusion.4 = (s32[1]{0:T(128)}, s32[1]{0:T(128)}) fusion(s32[2]{0:T(128)S(1)} %and_select_fusion), kind=kLoop, calls=%fused_computation.19 | loop fusion | bytes 16 | tf_op jit(solution)/shard_map/slice | solution.py:342
  33.2 0.1 collective-permute-start.5
  33.3 1.6 %collective-permute-done.7 = bf16[1,2,2,64,256]{4,3,2,1,0:T(8,128)(2,1)S(1)} collective-permute-done((bf16[1,2,2,64,256]{4,3,2,1,0:T(8,128)(2,1)S(1)}, bf16[1,2,2,64,256]{4,3,2,1,0:T(8,128)(2,1)S(1)}, u32[]{:S(2)}, u32[]{:S(2)}) %collective-permute-start.7) | collective-permute-done | bytes 131104 | tf_op jit(solution)/shard_map/ppermute | solution.py:313
  35.0 1.5 %collective-permute-start.10 = (bf16[1,2,2,64,256]{4,3,2,1,0:T(8,128)(2,1)S(1)}, bf16[1,2,2,64,256]{4,3,2,1,0:T(8,128)(2,1)S(1)}, u32[]{:S(2)}, u32[]{:S(2)}) collective-permute-start(bf16[1,2,2,64,256]{4,3,2,1,0:T(8,128)(2,1)S(1)} %fusion.2), channel_id=1, source_target_pairs={{0,2},{2,0},{1,3},{3,1},{4,6},{6,4},{5,7},{7,5},{8,10},{10,8},{9,1... | collective-permute-start | bytes 393224 | tf_op jit(solution)/shard_map/ppermute | solution.py:317
  36.4 1.1 %convert_add_fusion = f32[2,2,2,64,256]{4,3,2,1,0:T(8,128)S(1)} fusion(f32[2,2,2,64,256]{4,3,2,1,0:T(8,128)} %copy-done.2, bf16[2,2,2,64,256]{4,3,2,1,0:T(8,128)(2,1)S(1)} %collective-permute-done.8), kind=kLoop, calls=%fused_computation.4 | loop fusion | flops 262144 | bytes 1310720 | tf_op jit(solution)/shard_map/add | solution.py:362
  37.5 1.2 %collective-permute-start.9 = (bf16[1,2,2,64,256]{4,3,2,1,0:T(8,128)(2,1)S(1)}, bf16[1,2,2,64,256]{4,3,2,1,0:T(8,128)(2,1)S(1)}, u32[]{:S(2)}, u32[]{:S(2)}) collective-permute-start(bf16[1,2,2,64,256]{4,3,2,1,0:T(8,128)(2,1)S(1)} %slice.53), channel_id=1, source_target_pairs={{0,8},{4,12},{8,0},{12,4},{1,9},{5,13},{9,1},{13,5},{2,10},{6,14},... | collective-permute-start | bytes 393224 | tf_op jit(solution)/shard_map/ppermute | solution.py:313
  38.8 1.2 %collective-permute-done.10.refs_2_ = bf16[1,2,2,64,256]{4,3,2,1,0:T(8,128)(2,1)S(1)} collective-permute-done((bf16[1,2,2,64,256]{4,3,2,1,0:T(8,128)(2,1)S(1)}, bf16[1,2,2,64,256]{4,3,2,1,0:T(8,128)(2,1)S(1)}, u32[]{:S(2)}, u32[]{:S(2)}) %collective-permute-start.10) | collective-permute-done | bytes 131104 | tf_op jit(solution)/shard_map/ppermute | solution.py:317
  40.0 0.6 %choose_source.1 = bf16[1,2,2,64,256]{4,3,2,1,0:T(8,128)(2,1)S(1)} custom-call(s32[2,2]{1,0:T(2,128)S(1)} %copy-done.7, bf16[2,2,64,256]{3,2,1,0:T(8,128)(2,1)S(1)} %bitcast.12, bf16[1,2,2,64,256]{4,3,2,1,0:T(8,128)(2,1)S(1)} %collective-permute-done.10.refs_2_), custom_call_target="tpu_custom_call" | custom-call | tf_op jit(solution)/shard_map/choose_source/pallas_call | solution.py:228
  40.6 1.7 %collective-permute-start.11 = (bf16[1,2,2,64,256]{4,3,2,1,0:T(8,128)(2,1)S(1)}, bf16[1,2,2,64,256]{4,3,2,1,0:T(8,128)(2,1)S(1)}, u32[]{:S(2)}, u32[]{:S(2)}) collective-permute-start(bf16[1,2,2,64,256]{4,3,2,1,0:T(8,128)(2,1)S(1)} %choose_source.1), channel_id=1, source_target_pairs={{0,4},{4,0},{8,12},{12,8},{1,5},{5,1},{9,13},{13,9},{2,6},{6,2},{1... | collective-permute-start | bytes 393224 | tf_op jit(solution)/shard_map/ppermute | solution.py:313
  42.3 2.3 %collective-permute-start.12 = (bf16[1,2,2,64,256]{4,3,2,1,0:T(8,128)(2,1)S(1)}, bf16[1,2,2,64,256]{4,3,2,1,0:T(8,128)(2,1)S(1)}, u32[]{:S(2)}, u32[]{:S(2)}) collective-permute-start(bf16[1,2,2,64,256]{4,3,2,1,0:T(8,128)(2,1)S(1)} %choose_source.1), channel_id=1, source_target_pairs={{0,8},{4,12},{8,0},{12,4},{1,9},{5,13},{9,1},{13,5},{2,10},{6,14},... | collective-permute-start | bytes 393224 | tf_op jit(solution)/shard_map/ppermute | solution.py:313
  44.6 0.4 collective-permute-start.13
  45.1 2.4 %collective-permute-done.9 = bf16[1,2,2,64,256]{4,3,2,1,0:T(8,128)(2,1)S(1)} collective-permute-done((bf16[1,2,2,64,256]{4,3,2,1,0:T(8,128)(2,1)S(1)}, bf16[1,2,2,64,256]{4,3,2,1,0:T(8,128)(2,1)S(1)}, u32[]{:S(2)}, u32[]{:S(2)}) %collective-permute-start.9) | collective-permute-done | bytes 131104 | tf_op jit(solution)/shard_map/ppermute | solution.py:313
  47.4 0.8 %left_products.1 = bf16[1,2,2,64,256]{4,3,2,1,0:T(8,128)(2,1)S(1)} custom-call(s32[2,2]{1,0:T(2,128)S(1)} %copy-done.7, bf16[4,1,2,32,256]{4,3,2,1,0:T(8,128)(2,1)S(1)} %pad_maximum_fusion.refs_1_, bf16[4,1,2,32,256]{4,3,2,1,0:T(8,128)(2,1)S(1)} %collective-permute-done.5.refs_2_, bf16[2,2,64,256]{3,2,1,0:T(8,128)(2,1)S(1)} %bitcast.13, ...), custom_call_target="tpu_custom_call" | custom-call | tf_op jit(solution)/shard_map/left_products/pallas_call | solution.py:270
  48.3 6.4 %collective-permute-done.12 = bf16[1,2,2,64,256]{4,3,2,1,0:T(8,128)(2,1)S(1)} collective-permute-done((bf16[1,2,2,64,256]{4,3,2,1,0:T(8,128)(2,1)S(1)}, bf16[1,2,2,64,256]{4,3,2,1,0:T(8,128)(2,1)S(1)}, u32[]{:S(2)}, u32[]{:S(2)}) %collective-permute-start.12) | collective-permute-done | bytes 131104 | tf_op jit(solution)/shard_map/ppermute | solution.py:313
  54.7 0.4 conditional.1
  54.7 0.4 right_products.2
  55.0 0.6 %copy-done.6 = bf16[1,2,2,64,256]{4,3,2,1,0:T(8,128)(2,1)} copy-done((bf16[1,2,2,64,256]{4,3,2,1,0:T(8,128)(2,1)}, bf16[1,2,2,64,256]{4,3,2,1,0:T(8,128)(2,1)S(1)}, u32[]{:S(2)}) %copy-start.6) | copy-done | bytes 131096
  (26 shorter events, 0.2 us)
Async XLA Ops:
  0.0 4.9 %copy-start = (bf16[2,2,3,256,512]{4,3,2,1,0:T(8,128)(2,1)S(1)}, bf16[2,2,3,256,512]{4,3,2,1,0:T(8,128)(2,1)}, u32[]{:S(2)}) copy-start(bf16[2,2,3,256,512]{4,3,2,1,0:T(8,128)(2,1)} %refs_3_) | copy-start | bytes 9437188
  0.0 4.9 %copy-start.3 = (s32[2,3]{1,0:T(2,128)S(1)}, s32[2,3]{1,0:T(2,128)}, u32[]{:S(2)}) copy-start(s32[2,3]{1,0:T(2,128)} %refs_0_.4) | copy-start | bytes 76
  0.0 4.9 %copy-start.7 = (s32[2,2]{1,0:T(2,128)S(1)}, s32[2,2]{1,0:T(2,128)}, u32[]{:S(2)}) copy-start(s32[2,2]{1,0:T(2,128)} %refs_0_.6) | copy-start | bytes 52
  0.0 4.9 %copy-start.4 = (f32[4,4]{1,0:T(4,128)S(1)}, f32[4,4]{1,0:T(4,128)}, u32[]{:S(2)}) copy-start(f32[4,4]{1,0:T(4,128)} %refs_2_.2) | copy-start | bytes 196
  4.9 1.2 %copy-start.1 = (bf16[1,2,4,4,64,256]{5,4,3,2,1,0:T(8,128)(2,1)S(1)}, bf16[1,2,4,4,64,256]{5,4,3,2,1,0:T(8,128)(2,1)}, u32[]{:S(2)}) copy-start(bf16[1,2,4,4,64,256]{5,4,3,2,1,0:T(8,128)(2,1)} %refs_4_) | copy-start | bytes 3145732
  6.1 10.2 %copy-start.8 = (bf16[2,2,2,64,256]{4,3,2,1,0:T(8,128)(2,1)S(1)}, bf16[2,2,2,64,256]{4,3,2,1,0:T(8,128)(2,1)}, u32[]{:S(2)}) copy-start(bf16[2,2,2,64,256]{4,3,2,1,0:T(8,128)(2,1)} %get-tuple-element.65) | copy-start | bytes 786436
  6.1 21.0 %copy-start.5 = (f32[2,2,2,64,256]{4,3,2,1,0:T(8,128)S(1)}, f32[2,2,2,64,256]{4,3,2,1,0:T(8,128)}, u32[]{:S(2)}) copy-start(f32[2,2,2,64,256]{4,3,2,1,0:T(8,128)} %get-tuple-element.64) | copy-start | bytes 1572868
  9.9 0.8 %copy-start.2 = (f32[2,2,2,64,256]{4,3,2,1,0:T(8,128)}, f32[2,2,2,64,256]{4,3,2,1,0:T(8,128)S(1)}, u32[]{:S(2)}) copy-start(f32[2,2,2,64,256]{4,3,2,1,0:T(8,128)S(1)} %get-tuple-element.66) | copy-start | bytes 1572868
  10.7 25.7 %collective-permute-start.8 = (bf16[2,2,2,64,256]{4,3,2,1,0:T(8,128)(2,1)S(1)}, bf16[2,2,2,64,256]{4,3,2,1,0:T(8,128)(2,1)S(1)}, u32[]{:S(2)}, u32[]{:S(2)}) collective-permute-start(bf16[2,2,2,64,256]{4,3,2,1,0:T(8,128)(2,1)S(1)} %get-tuple-element.67), channel_id=1, source_target_pairs={{0,4},{4,0},{8,12},{12,8},{1,5},{5,1},{9,13},{13,9},{2,6},{6,2},{1... | collective-permute-start | bytes 786440 | tf_op jit(solution)/shard_map/ppermute | solution.py:313
  13.8 7.4 %collective-permute-start.3 = (bf16[1,1,2,32,256]{4,3,2,1,0:T(8,128)(2,1)S(1)}, bf16[1,1,2,32,256]{4,3,2,1,0:T(8,128)(2,1)S(1)}, u32[]{:S(2)}, u32[]{:S(2)}) collective-permute-start(bf16[1,1,2,32,256]{4,3,2,1,0:T(8,128)(2,1)S(1)} %bitcast.14), channel_id=1, source_target_pairs={{0,8},{4,12},{8,0},{12,4},{1,9},{5,13},{9,1},{13,5},{2,10},{6,14},... | collective-permute-start | bytes 98312 | tf_op jit(solution)/shard_map/ppermute | solution.py:313
  16.4 10.7 %collective-permute-start.6 = (bf16[2,2,2,64,256]{4,3,2,1,0:T(8,128)(2,1)S(1)}, bf16[2,2,2,64,256]{4,3,2,1,0:T(8,128)(2,1)S(1)}, u32[]{:S(2)}, u32[]{:S(2)}) collective-permute-start(bf16[2,2,2,64,256]{4,3,2,1,0:T(8,128)(2,1)S(1)} %copy-done.8), channel_id=1, source_target_pairs={{0,4},{4,0},{8,12},{12,8},{1,5},{5,1},{9,13},{13,9},{2,6},{6,2},{1... | collective-permute-start | bytes 786440 | tf_op jit(solution)/shard_map/ppermute | solution.py:313
  21.2 12.0 %collective-permute-start.4 = (bf16[2,1,2,32,256]{4,3,2,1,0:T(8,128)(2,1)S(1)}, bf16[2,1,2,32,256]{4,3,2,1,0:T(8,128)(2,1)S(1)}, u32[]{:S(2)}, u32[]{:S(2)}) collective-permute-start(bf16[2,1,2,32,256]{4,3,2,1,0:T(8,128)(2,1)S(1)} %pad_maximum_fusion.1), channel_id=1, source_target_pairs={{0,4},{4,0},{8,12},{12,8},{1,5},{5,1},{9,13},{13,9},{2,6},{6,2},{1... | collective-permute-start | bytes 196616 | tf_op jit(solution)/shard_map/ppermute | solution.py:313
  27.2 7.7 %collective-permute-start.7 = (bf16[1,2,2,64,256]{4,3,2,1,0:T(8,128)(2,1)S(1)}, bf16[1,2,2,64,256]{4,3,2,1,0:T(8,128)(2,1)S(1)}, u32[]{:S(2)}, u32[]{:S(2)}) collective-permute-start(bf16[1,2,2,64,256]{4,3,2,1,0:T(8,128)(2,1)S(1)} %slice.54), channel_id=1, source_target_pairs={{0,8},{4,12},{8,0},{12,4},{1,9},{5,13},{9,1},{13,5},{2,10},{6,14},... | collective-permute-start | bytes 393224 | tf_op jit(solution)/shard_map/ppermute | solution.py:313
  33.2 11.8 %collective-permute-start.5 = (bf16[4,1,2,32,256]{4,3,2,1,0:T(8,128)(2,1)S(1)}, bf16[4,1,2,32,256]{4,3,2,1,0:T(8,128)(2,1)S(1)}, u32[]{:S(2)}, u32[]{:S(2)}) collective-permute-start(bf16[4,1,2,32,256]{4,3,2,1,0:T(8,128)(2,1)S(1)} %pad_maximum_fusion.refs_1_), channel_id=1, source_target_pairs={{0,1},{1,0},{2,3},{3,2},{4,5},{5,4},{6,7},{7,6},{8,9},{9,8},{10,11... | collective-permute-start | bytes 393224 | tf_op jit(solution)/shard_map/ppermute | solution.py:317
  35.0 5.0 %collective-permute-start.10 = (bf16[1,2,2,64,256]{4,3,2,1,0:T(8,128)(2,1)S(1)}, bf16[1,2,2,64,256]{4,3,2,1,0:T(8,128)(2,1)S(1)}, u32[]{:S(2)}, u32[]{:S(2)}) collective-permute-start(bf16[1,2,2,64,256]{4,3,2,1,0:T(8,128)(2,1)S(1)} %fusion.2), channel_id=1, source_target_pairs={{0,2},{2,0},{1,3},{3,1},{4,6},{6,4},{5,7},{7,5},{8,10},{10,8},{9,1... | collective-permute-start | bytes 393224 | tf_op jit(solution)/shard_map/ppermute | solution.py:317
  37.5 9.9 %collective-permute-start.9 = (bf16[1,2,2,64,256]{4,3,2,1,0:T(8,128)(2,1)S(1)}, bf16[1,2,2,64,256]{4,3,2,1,0:T(8,128)(2,1)S(1)}, u32[]{:S(2)}, u32[]{:S(2)}) collective-permute-start(bf16[1,2,2,64,256]{4,3,2,1,0:T(8,128)(2,1)S(1)} %slice.53), channel_id=1, source_target_pairs={{0,8},{4,12},{8,0},{12,4},{1,9},{5,13},{9,1},{13,5},{2,10},{6,14},... | collective-permute-start | bytes 393224 | tf_op jit(solution)/shard_map/ppermute | solution.py:313
  40.6 7.7 %collective-permute-start.11 = (bf16[1,2,2,64,256]{4,3,2,1,0:T(8,128)(2,1)S(1)}, bf16[1,2,2,64,256]{4,3,2,1,0:T(8,128)(2,1)S(1)}, u32[]{:S(2)}, u32[]{:S(2)}) collective-permute-start(bf16[1,2,2,64,256]{4,3,2,1,0:T(8,128)(2,1)S(1)} %choose_source.1), channel_id=1, source_target_pairs={{0,4},{4,0},{8,12},{12,8},{1,5},{5,1},{9,13},{13,9},{2,6},{6,2},{1... | collective-permute-start | bytes 393224 | tf_op jit(solution)/shard_map/ppermute | solution.py:313
  42.3 12.3 %collective-permute-start.12 = (bf16[1,2,2,64,256]{4,3,2,1,0:T(8,128)(2,1)S(1)}, bf16[1,2,2,64,256]{4,3,2,1,0:T(8,128)(2,1)S(1)}, u32[]{:S(2)}, u32[]{:S(2)}) collective-permute-start(bf16[1,2,2,64,256]{4,3,2,1,0:T(8,128)(2,1)S(1)} %choose_source.1), channel_id=1, source_target_pairs={{0,8},{4,12},{8,0},{12,4},{1,9},{5,13},{9,1},{13,5},{2,10},{6,14},... | collective-permute-start | bytes 393224 | tf_op jit(solution)/shard_map/ppermute | solution.py:313
  44.6 10.1 %collective-permute-start.13 = (bf16[1,2,2,64,256]{4,3,2,1,0:T(8,128)(2,1)S(1)}, bf16[1,2,2,64,256]{4,3,2,1,0:T(8,128)(2,1)S(1)}, u32[]{:S(2)}, u32[]{:S(2)}) collective-permute-start(bf16[1,2,2,64,256]{4,3,2,1,0:T(8,128)(2,1)S(1)} %choose_source.1), channel_id=1, source_target_pairs={{0,12},{4,8},{8,4},{12,0},{1,13},{5,9},{9,5},{13,1},{2,14},{6,10},... | collective-permute-start | bytes 393224 | tf_op jit(solution)/shard_map/ppermute | solution.py:313
  55.0 0.7 %copy-start.6 = (bf16[1,2,2,64,256]{4,3,2,1,0:T(8,128)(2,1)}, bf16[1,2,2,64,256]{4,3,2,1,0:T(8,128)(2,1)S(1)}, u32[]{:S(2)}) copy-start(bf16[1,2,2,64,256]{4,3,2,1,0:T(8,128)(2,1)S(1)} %get-tuple-element.99) | copy-start | bytes 393220
